TPU v7x, 32 devices: a whole 2x2x4 slice. The times are simulated.
32 devices in a mesh: seq: 8 (over z, core), grp: 2 (over y), dp: 2 (over x).
Axes of the slice: x: 2, y: 2, z: 4, core: 2. Of those that a mesh axis runs over, the one named last changes fastest.
Arguments:
- clips: bfloat16 [2, 1024, 1408], P('dp', 'seq'), may hold values from -6 to 6
- context: int32 [2, 1024], P('dp', 'seq'), may hold values from 0 to 1, as said below
- predict_index: int32 [2, 1536], P('dp', 'seq'), may hold values from -1 to 1023, as said below
- target_qkv: bfloat16 [3, 1408, 1408], P(None, 'dp', 'grp'), may hold values from -8 to 8
- target_out: bfloat16 [1408, 1408], P('grp'), may hold values from -0.15625 to 0.15625
- student_qkv: bfloat16 [3, 1408, 1408], P(None, 'dp', 'grp'), may hold values from -8 to 8
- student_out: bfloat16 [1408, 1408], P('grp', 'dp'), may hold values from -0.15625 to 0.15625
- mask_token: float32 [1408], replicated, may hold values from -4 to 4
Outputs:
- out_grad: float32 [1408, 1408], P('grp', 'dp')
- target_blend: float32 [1408, 1408], P('grp')
Inputs may be any that keep to these rules, and one draw needn't show every extreme that they name: In every aligned block of 128 tokens of a clip exactly 32 tokens have context 1 and the others 0. `predict_index`: each device's 192 slots name distinct target positions (context 0) of its clip, followed by -1 in the unused slots; different devices' lists may name the same position. In every clip one list is full.
All inputs are finite; a program needn't handle non-finite values.
Results may differ from a plain program's by a relative error of at most 0.014.
Values may be sent and summed in bfloat16 or wider, within the bound.
A program may use at most 128 MiB of HBM per device.

v0:
```python
import math

import jax
import jax.numpy as jnp
from jax import lax
from jax.sharding import PartitionSpec as P

HEAD_DIM = 88
CTX_DEV = 32


EPSILON = 1e-06
MOMENTUM = 0.99


def layer_norm(values):
    center = values - jnp.mean(values, axis=-1, keepdims=True)
    factor = lax.rsqrt(jnp.mean(center * center, axis=-1, keepdims=True) + EPSILON)
    return (center * factor, factor)


def position_table(places, width):
    half_width = width // 2
    spacing = jnp.exp(jnp.arange(half_width, dtype=jnp.float32) * (-math.log(10000.0) / half_width))
    angles = places.astype(jnp.float32)[:, None] * spacing[None, :]
    return jnp.concatenate([jnp.sin(angles), jnp.cos(angles)], axis=1)


def to_heads(queries):
    head_count = queries.shape[1] // HEAD_DIM
    return queries.reshape(queries.shape[0], head_count, HEAD_DIM).transpose(1, 0, 2)


def empty_state(head_count, row_count):
    peaks = jnp.full((head_count, row_count), -1e30, jnp.float32)
    totals = jnp.zeros((head_count, row_count), jnp.float32)
    summed = jnp.zeros((head_count, row_count, HEAD_DIM), jnp.float32)
    return (peaks, totals, summed)


def from_heads(running):
    peaks, totals, summed = running
    mixed = summed / totals[:, :, None]
    head_count, row_count, unused = mixed.shape
    return mixed.transpose(1, 0, 2).reshape(row_count, head_count * HEAD_DIM).astype(jnp.bfloat16)


def attend_shard(running, shard_rows, query_heads):
    peaks, totals, summed = running
    key_rows, value_rows = shard_rows
    length = key_rows.shape[0]
    head_count = query_heads.shape[0]
    key_heads = key_rows.reshape(length, head_count, HEAD_DIM)
    value_heads = value_rows.reshape(length, head_count, HEAD_DIM)
    factor = HEAD_DIM ** (-0.5)
    scores = (
        jnp.einsum("hqd,khd->hqk", query_heads, key_heads, preferred_element_type=jnp.float32)
        * factor
    )
    raised = jnp.maximum(peaks, jnp.max(scores, axis=2))
    shifted = jnp.exp(scores - raised[:, :, None])
    totals = jnp.sum(shifted, axis=2)
    summed = jnp.einsum(
        "hqk,khd->hqd",
        shifted.astype(jnp.bfloat16),
        value_heads,
        preferred_element_type=jnp.float32,
    )
    return (raised, totals, summed)


def body(
    clips, context, predict_index, target_qkv, target_out, student_qkv, student_out, mask_token
):
    tokens = clips[0]
    keep_flags = context[0]
    listed = predict_index[0]
    row_count, width = tokens.shape
    half_width = target_qkv.shape[2]
    head_count = half_width // HEAD_DIM
    normed = layer_norm(tokens.astype(jnp.float32))[0].astype(jnp.bfloat16)
    projected = jnp.einsum(
        "nr,krc->knc",
        normed,
        lax.all_gather(target_qkv, "dp", axis=1, tiled=True),
        preferred_element_type=jnp.float32,
    )
    projected = projected.astype(jnp.bfloat16)
    target_state = attend_shard(
        empty_state(head_count, row_count),
        (
            lax.all_gather(projected[1], "seq", axis=0, tiled=True),
            lax.all_gather(projected[2], "seq", axis=0, tiled=True),
        ),
        query_heads=to_heads(projected[0]),
    )
    target_mixed = from_heads(target_state)
    target_part = jnp.dot(target_mixed, target_out, preferred_element_type=jnp.float32)
    target_sum = lax.psum(target_part.astype(jnp.bfloat16), "grp").astype(jnp.float32)
    features = layer_norm(tokens.astype(jnp.float32) + target_sum)[0].astype(jnp.bfloat16)
    first_row = lax.axis_index("seq") * row_count
    every_list = lax.all_gather(listed, "seq", axis=0, tiled=True)
    places = first_row + jnp.arange(row_count, dtype=jnp.int32)
    usable = jnp.sum((every_list[None, :] == places[:, None]).astype(jnp.float32), axis=1)
    slot_count = places.shape[0]
    is_context = keep_flags == 1
    context_order = jnp.cumsum(is_context.astype(jnp.int32)) - 1
    selector = (
        (context_order[None, :] == jnp.arange(CTX_DEV, dtype=jnp.int32)[:, None])
        & is_context[None, :]
    ).astype(jnp.bfloat16)
    context_rows = jnp.dot(selector, normed, preferred_element_type=jnp.float32).astype(
        jnp.bfloat16
    )
    seeds = mask_token[None, :] + position_table(jnp.maximum(places, 0), width)
    seed_normed = layer_norm(seeds)[0].astype(jnp.bfloat16)
    shard_rows = lax.all_gather(student_qkv, "dp", axis=1, tiled=True)
    query_total = jnp.dot(seed_normed, shard_rows[0], preferred_element_type=jnp.float32)
    pair_total = jnp.einsum(
        "nr,krc->knc", context_rows, shard_rows[1:], preferred_element_type=jnp.float32
    )
    student_pairs = pair_total
    student_pairs = student_pairs.astype(jnp.bfloat16)
    student_state = attend_shard(
        empty_state(head_count, slot_count),
        (
            lax.all_gather(student_pairs[0], "seq", axis=0, tiled=True),
            lax.all_gather(student_pairs[1], "seq", axis=0, tiled=True),
        ),
        query_heads=to_heads(query_total.astype(jnp.bfloat16)),
    )
    student_mixed = from_heads(student_state)
    relaid = lax.all_gather(student_out, "dp", axis=1, tiled=True)
    student_part = jnp.dot(student_mixed, relaid, preferred_element_type=jnp.float32)
    student_sum = lax.psum(student_part.astype(jnp.bfloat16), "grp").astype(jnp.float32)
    predicted, factor = layer_norm(seeds + student_sum)
    wanted = features.astype(jnp.float32)
    slope = jnp.clip(predicted - wanted, -1.0, 1.0) * usable[:, None]
    back_grad = (
        slope
        - jnp.mean(slope, axis=1, keepdims=True)
        - predicted * jnp.mean(slope * predicted, axis=1, keepdims=True)
    ) * factor
    local_grad = jnp.dot(
        student_mixed.astype(jnp.float32).T, back_grad, precision=lax.Precision.HIGHEST
    )
    column_grad = lax.psum_scatter(
        local_grad.astype(jnp.bfloat16), "dp", scatter_dimension=1, tiled=True
    )
    out_grad = lax.psum(column_grad, "seq").astype(jnp.float32)
    target_blend = MOMENTUM * target_out.astype(jnp.float32) + (1.0 - MOMENTUM) * relaid.astype(
        jnp.float32
    )
    return (out_grad, target_blend)


def solution(mesh):
    in_specs = (
        P("dp", "seq", None),
        P("dp", "seq"),
        P("dp", "seq"),
        P(None, "dp", "grp"),
        P("grp", None),
        P(None, "dp", "grp"),
        P("grp", "dp"),
        P(),
    )
    out_specs = (P("grp", "dp"), P("grp", None))
    return jax.shard_map(body, mesh=mesh, in_specs=in_specs, out_specs=out_specs, check_vma=False)
```

profile of v0, /device:TPU:0, one launch (start us, length us, event | category | flops | bytes accessed | tf_op | source)
XLA Modules:
  0.0 480.1 jit_solution(4295476264770077709)
XLA Ops:
  7.2 6.9 %copy.48 = bf16[3,704,704]{2,0,1:T(4,128)(2,1)} copy(bf16[3,704,704]{2,1,0:T(8,128)(2,1)} %param.11) | data formatting | bytes 5947392 | tf_op args[3]
  14.2 4.8 %copy.41 = bf16[3,704,704]{2,0,1:T(4,128)(2,1)} copy(bf16[3,704,704]{2,1,0:T(8,128)(2,1)S(1)} %copy-done.5) | data formatting | bytes 5947392 | tf_op args[5]
  22.2 104.2 %all-gather.15.cloned.1.call-done = bf16[3,1408,704]{2,0,1:T(4,128)(2,1)} async-done(((bf16[3,704,704]{2,0,1:T(4,128)(2,1)}), bf16[3,1408,704]{2,0,1:T(4,128)(2,1)}) %all-gather.15.cloned.1.call-update) | async-done | bytes 5947408 | tf_op jit(solution)/shard_map/all_gather | solution.py:85
  126.4 6.0 %fusion.16 = bf16[3,128,704]{1,2,0:T(8,128)(2,1)S(1)} fusion(bf16[3,1408,704]{2,0,1:T(4,128)(2,1)} %all-gather.15.cloned.1.call-done, bf16[1,128,1408]{2,1,0:T(8,128)(2,1)S(1)} %copy-done.1, f32[128]{0:T(128)S(1)} %add_rsqrt_fusion.2, f32[128]{0:T(128)S(1)} %broadcast_multiply_fusion.4), kind=kOutput, calls=%fused_computation.21 | convolution fusion | flops 762257408 | bytes 6849536 | tf_op jit(solution)/shard_map/nr,krc->knc/dot_general | solution.py:82
  135.9 101.4 %all-gather.11.cloned.1.call-done = bf16[3,1408,704]{2,0,1:T(4,128)(2,1)} async-done(((bf16[3,704,704]{2,0,1:T(4,128)(2,1)}), bf16[3,1408,704]{2,0,1:T(4,128)(2,1)}) %all-gather.11.cloned.1.call-update) | async-done | bytes 5947408 | tf_op jit(solution)/shard_map/all_gather | solution.py:117
  237.3 7.6 %slice.29 = bf16[2,1408,704]{2,0,1:T(2,128)(2,1)} slice(bf16[3,1408,704]{2,0,1:T(4,128)(2,1)} %all-gather.11.cloned.1.call-done), slice={[1:3], [0:1408], [0:704]} | slice | bytes 7929856 | tf_op jit(solution)/shard_map/slice | solution.py:120
  244.9 3.7 fusion.30
  249.3 14.5 %all-gather.1 = bf16[1,256,704]{2,1,0:T(8,128)(2,1)S(1)} all-gather(bf16[1,32,704]{2,1,0:T(8,128)(2,1)S(1)} %get-tuple-element.19), channel_id=3, replica_groups=mesh['seq'=8,'grp'=2,'dp'=2] {'seq'}, dimensions={1}, use_global_device_ids=true | all-gather | bytes 405504 | tf_op jit(solution)/shard_map/all_gather | solution.py:128
  264.7 7.1 %slice.28 = bf16[1,1408,704]{2,0,1:T(2,128)(2,1)} slice(bf16[3,1408,704]{2,0,1:T(4,128)(2,1)} %all-gather.11.cloned.1.call-done), slice={[0:1], [0:1408], [0:704]} | slice | bytes 3964928 | tf_op jit(solution)/shard_map/slice | solution.py:118
  271.7 12.0 %copy.54 = bf16[1,1408,704]{1,2,0:T(8,128)(2,1)S(1)} copy(bf16[1,1408,704]{2,0,1:T(2,128)(2,1)} %slice.28) | data formatting | bytes 3964928
  283.8 16.5 %all-gather = bf16[1,256,704]{2,1,0:T(8,128)(2,1)S(1)} all-gather(bf16[1,32,704]{2,1,0:T(8,128)(2,1)} %get-tuple-element.18), channel_id=2, replica_groups=mesh['seq'=8,'grp'=2,'dp'=2] {'seq'}, dimensions={1}, use_global_device_ids=true | all-gather | bytes 405504 | tf_op jit(solution)/shard_map/all_gather | solution.py:127
  304.3 3.2 convolution_convert_fusion.2
  312.5 18.5 %all-gather.19.cloned.1.call-done = bf16[1,1024,704]{1,2,0:T(8,128)(2,1)} async-done(((bf16[1,128,704]{1,2,0:T(8,128)(2,1)}), bf16[1,1024,704]{1,2,0:T(8,128)(2,1)}) %all-gather.19.cloned.1.call-update) | async-done | bytes 1441808 | tf_op jit(solution)/shard_map/all_gather | solution.py:93
  331.0 3.6 fusion.36
  337.6 7.6 %all-reduce = s32[1536]{0:T(1024)S(1)} all-reduce(s32[1536]{0:T(1024)S(1)} %dynamic-update-slice), channel_id=6, replica_groups=mesh['seq'=8,'grp'=2,'dp'=2] {'seq'}, use_global_device_ids=true, to_apply=%add | all-reduce | flops 1536 | bytes 12288
  345.4 22.1 %all-reduce.7.cloned.1.call-done = (bf16[128,1408]{1,0:T(8,128)(2,1)}, bf16[128,1408]{1,0:T(8,128)(2,1)}) async-done(((bf16[128,1408]{1,0:T(8,128)(2,1)}, bf16[128,1408]{1,0:T(8,128)(2,1)}), (bf16[128,1408]{1,0:T(8,128)(2,1)}, bf16[128,1408]{1,0:T(8,128)(2,1)})) %all-reduce.7.cloned.1.call-update) | async-done | bytes 720912 | tf_op jit(solution)/shard_map/psum | solution.py:99
  373.0 2.5 copy.52
  375.6 4.1 copy.50
  379.7 28.6 %reduce-scatter.4.cloned.1.call-done = bf16[704,704]{1,0:T(8,128)(2,1)} async-done(((bf16[1408,704]{1,0:T(8,128)(2,1)}), bf16[704,704]{1,0:T(8,128)(2,1)}) %reduce-scatter.4.cloned.1.call-update) | async-done | bytes 991248
  408.3 2.3 copy.53
  410.7 4.3 multiply_add_fusion
  415.0 5.6 %copy.51 = f32[704,1408]{1,0:T(8,128)} copy(f32[704,1408]{0,1:T(8,128)} %multiply_add_fusion) | data formatting | bytes 7929856
  420.6 49.9 %all-reduce.5.cloned.1.call-done = bf16[704,704]{1,0:T(8,128)(2,1)} async-done(((bf16[704,704]{1,0:T(8,128)(2,1)}), bf16[704,704]{1,0:T(8,128)(2,1)}) %all-reduce.5.cloned.1.call-update) | async-done | bytes 991248 | tf_op jit(solution)/shard_map/psum | solution.py:150
  470.5 2.7 convert_element_type.121
  (89 shorter events, 25.1 us)
Async XLA Ops:
  7.2 7.1 %copy-start.5 = (bf16[3,704,704]{2,1,0:T(8,128)(2,1)S(1)}, bf16[3,704,704]{2,1,0:T(8,128)(2,1)}, u32[]{:S(2)}) copy-start(bf16[3,704,704]{2,1,0:T(8,128)(2,1)} %param.13) | copy-start | bytes 8921092
  7.2 119.2 %all-gather.15.cloned.1.call-start = ((), (), s32[]{:S(2)}) async-start(), calls=%async_computation.3 | async-start | bytes 12976128 | tf_op jit(solution)/shard_map/all_gather | solution.py:85
  14.2 223.2 %all-gather.11.cloned.1.call-start = ((), (), s32[]{:S(2)}) async-start(), calls=%async_computation.1 | async-start | bytes 12976128 | tf_op jit(solution)/shard_map/all_gather | solution.py:117
  19.0 1.2 copy-start.6
  19.0 2.8 copy-start.1
  19.1 285.2 %all-gather.13.cloned.1.call-start = ((), (), s32[]{:S(2)}) async-start(), calls=%async_computation.2 | async-start | bytes 3244032 | tf_op jit(solution)/shard_map/all_gather | solution.py:133
  21.8 285.7 %all-gather.17.cloned.1.call-start = ((), (), s32[]{:S(2)}) async-start(), calls=%async_computation.5 | async-start | bytes 1622016 | tf_op jit(solution)/shard_map/all_gather | solution.py:92
  22.2 111.3 %copy-start.11 = (s32[1,128]{1,0:T(1,128)S(1)}, s32[1,128]{1,0:T(1,128)}, u32[]{:S(2)}) copy-start(s32[1,128]{1,0:T(1,128)} %param.9) | copy-start | bytes 1540
  22.2 113.1 %copy-start.9 = (f32[1408]{0:T(1024)S(1)}, f32[1408]{0:T(1024)}, u32[]{:S(2)}) copy-start(f32[1408]{0:T(1024)} %param.15) | copy-start | bytes 16900
  133.2 197.8 %all-gather.19.cloned.1.call-start = ((), (), s32[]{:S(2)}) async-start(), calls=%async_computation.6 | async-start | bytes 1622016 | tf_op jit(solution)/shard_map/all_gather | solution.py:93
  283.8 83.8 %all-reduce.7.cloned.1.call-start = ((), (), s32[]{:S(2)}) async-start(), calls=%async_computation.8 | async-start | bytes 1441792 | tf_op jit(solution)/shard_map/psum | solution.py:99
  301.2 2.6 copy-start.8
  302.0 5.5 %copy-start.7 = (bf16[1,128,704]{1,2,0:T(8,128)(2,1)S(1)}, bf16[1,128,704]{1,2,0:T(8,128)(2,1)}, u32[]{:S(2)}) copy-start(bf16[1,128,704]{1,2,0:T(8,128)(2,1)} %get-tuple-element.17) | copy-start | bytes 540676
  309.7 1.9 copy-start
  312.5 22.2 %copy-start.3 = (bf16[704,1408]{1,0:T(8,128)(2,1)S(1)}, bf16[704,1408]{1,0:T(8,128)(2,1)}, u32[]{:S(2)}) copy-start(bf16[704,1408]{1,0:T(8,128)(2,1)} %param.12) | copy-start | bytes 5947396
  331.0 5.0 %copy-start.12 = (u32[32]{0:T(128)S(1)}, u32[32]{0:T(128)}, u32[]{:S(2)}) copy-start(u32[32]{0:T(128)} %constant.55) | copy-start | bytes 388
  331.0 6.3 %copy-start.10 = (s32[1,192]{1,0:T(1,128)S(1)}, s32[1,192]{1,0:T(1,128)}, u32[]{:S(2)}) copy-start(s32[1,192]{1,0:T(1,128)} %param.10) | copy-start | bytes 2308
  336.0 72.4 %reduce-scatter.4.cloned.1.call-start = ((), (), s32[]{:S(2)}) async-start(), calls=%async_computation.7 | async-start | bytes 3244032
  367.6 2.9 copy-start.4
  375.5 35.1 %copy-start.2 = (bf16[704,1408]{0,1:T(8,128)(2,1)S(1)}, bf16[704,1408]{0,1:T(8,128)(2,1)}, u32[]{:S(2)}) copy-start(bf16[704,1408]{0,1:T(8,128)(2,1)} %all-gather.13.cloned.1.call-done) | copy-start | bytes 5947396
  375.5 95.0 %all-reduce.5.cloned.1.call-start = ((), (), s32[]{:S(2)}) async-start(), calls=%async_computation.4 | async-start | bytes 2162688 | tf_op jit(solution)/shard_map/psum | solution.py:150
Sparse Core Ops, SparseCore 0:
  14.3 112.0 all-gather.14
  128.0 109.3 all-gather.10
  239.5 33.8 all-gather.12
  274.8 28.2 all-gather.16
  304.5 26.4 all-gather.18
  336.1 31.4 all-reduce.6
  375.7 32.6 reduce-scatter.3
  411.2 59.2 all-reduce.4
where the time goes:
time: 481 us; the launch traced here: 480 us
  waiting for transfers between devices  325 us (68%)
  local copies, waits for them, and re-layouts  61.8 us (13%)
  blocking collectives  38.6 us (8%)
  matrix products  24.5 us (5%)
  between operations  15.1 us (3%)
  other arithmetic  14.7 us (3%)
    all_gather x1, waiting for transfers between devices, body(): lax.all_gather(target_qkv, 'dp', axis=1, tiled=True)  104 us
    all_gather x1, waiting for transfers between devices, body(): shard_rows = lax.all_gather(student_qkv, 'dp', axis=1, tiled=True)  101 us
    psum x1, waiting for transfers between devices, body(): out_grad = lax.psum(column_grad, 'seq').astype(jnp.float32)  49.9 us
    unnamed x37, local copies, waits for them, and re-layouts  43.8 us
    unnamed x9, waiting for transfers between devices  28.7 us
    psum x1, waiting for transfers between devices, body(): lax.psum(target_part.astype(jnp.bfloat16), 'grp').astype(jnp.float32)  22.1 us
    all_gather x1, waiting for transfers between devices, body(): lax.all_gather(projected[2], 'seq', axis=0, tiled=True)  18.5 us
    all_gather x1, blocking collectives, body(): lax.all_gather(student_pairs[0], 'seq', axis=0, tiled=True)  16.5 us
  transfers between devices with their start and end apart: 8, of which 6 were waited for; matrix products, arithmetic and copies ran while one was open for 15% of the time, Pallas kernels for 0%

commit v1 on v0

v1 whole, which is shorter than its diff:
```python
import math

import jax
import jax.numpy as jnp
from jax import lax
from jax.sharding import PartitionSpec as P

HEAD_DIM = 88
CTX_DEV = 32
EPSILON = 1e-06
MOMENTUM = 0.99
STRIDE = 32


def layer_norm(values):
    center = values - jnp.mean(values, axis=-1, keepdims=True)
    factor = lax.rsqrt(jnp.mean(center * center, axis=-1, keepdims=True) + EPSILON)
    return (center * factor, factor)


def position_table(length, width):
    half_width = width // 2
    spacing = jnp.exp(jnp.arange(half_width, dtype=jnp.float32) * (-math.log(10000.0) / half_width))
    high = (jnp.arange(length // STRIDE) * STRIDE).astype(jnp.float32)[:, None] * spacing[None, :]
    low = jnp.arange(STRIDE).astype(jnp.float32)[:, None] * spacing[None, :]
    sin_h, cos_h = jnp.sin(high), jnp.cos(high)
    sin_l, cos_l = jnp.sin(low), jnp.cos(low)
    first = jnp.concatenate([sin_h, cos_h], axis=1)
    second = jnp.concatenate([cos_h, -sin_h], axis=1)
    twice_c = jnp.concatenate([cos_l, cos_l], axis=1)
    twice_s = jnp.concatenate([sin_l, sin_l], axis=1)
    table = first[:, None, :] * twice_c[None] + second[:, None, :] * twice_s[None]
    return table.reshape(length, width)


def attend(queries, keys, values):
    scores = lax.dot_general(
        queries, keys, (((1,), (1,)), ((), ())), preferred_element_type=jnp.float32
    ) * (HEAD_DIM ** (-0.5))
    shifted = jnp.exp(scores - jnp.max(scores, axis=1, keepdims=True))
    totals = jnp.sum(shifted, axis=1, keepdims=True)
    summed = jnp.dot(shifted.astype(jnp.bfloat16), values, preferred_element_type=jnp.float32)
    return (summed / totals).astype(jnp.bfloat16)


def dot32(left, right):
    return jnp.dot(left, right, preferred_element_type=jnp.float32)


def both_of_dp(block, axis):
    if lax.axis_size("dp") != 2:
        return lax.all_gather(block, "dp", axis=axis, tiled=True)
    other = lax.ppermute(block, "dp", [(0, 1), (1, 0)])
    first = lax.axis_index("dp") == 0
    return jnp.concatenate(
        [jnp.where(first, block, other), jnp.where(first, other, block)], axis=axis
    )


def body(
    clips, context, predict_index, target_qkv, target_out, student_qkv, student_out, mask_token
):
    tokens = clips[0].astype(jnp.float32)
    row_count, width = tokens.shape
    half_width = target_qkv.shape[2]
    head_count = half_width // HEAD_DIM
    shards = lax.axis_size("seq")
    rep = shards // head_count
    length = shards * row_count
    me = lax.axis_index("seq")
    head, part = me // rep, me % rep
    part_rows = length // rep

    def columns(weights):
        return lax.dynamic_slice_in_dim(weights, head * HEAD_DIM, HEAD_DIM, axis=2)

    mine = jnp.concatenate([columns(target_qkv), columns(student_qkv)], axis=0)
    mine = jnp.concatenate([mine[k] for k in range(6)], axis=1)
    weights = both_of_dp(mine, 0)
    relaid = both_of_dp(student_out, 1)

    normed = layer_norm(tokens)[0].astype(jnp.bfloat16)
    every = lax.all_gather(normed, "seq", axis=0, tiled=True)
    small = lax.all_gather(jnp.concatenate([context[0], predict_index[0]]), "seq", axis=0)
    flags, lists = small[:, :row_count], small[:, row_count:].reshape(-1)

    seeds = mask_token[None, :] + position_table(length, width)
    seed_normed = layer_norm(seeds)[0].astype(jnp.bfloat16)

    def own_part(rows):
        if rep == 1:
            return rows
        return lax.dynamic_slice_in_dim(rows, part * part_rows, part_rows, axis=0)

    pick = lambda k: weights[:, k * HEAD_DIM : (k + 1) * HEAD_DIM]
    seed_queries = dot32(own_part(seed_normed), pick(3)).astype(jnp.bfloat16)
    if rep == 1:
        triple = dot32(every, weights[:, : 3 * HEAD_DIM]).astype(jnp.bfloat16)
        query_t = triple[:, :HEAD_DIM]
        pair_t = triple[:, HEAD_DIM:]
    else:
        query_t = dot32(own_part(every), pick(0)).astype(jnp.bfloat16)
        pair_t = dot32(every, weights[:, HEAD_DIM : 3 * HEAD_DIM]).astype(jnp.bfloat16)
    target_mixed = attend(query_t, pair_t[:, :HEAD_DIM], pair_t[:, HEAD_DIM:])

    is_context = flags == 1
    order = jnp.cumsum(is_context.astype(jnp.int32), axis=1) - 1
    selector = (
        (order[:, None, :] == jnp.arange(CTX_DEV, dtype=jnp.int32)[None, :, None])
        & is_context[:, None, :]
    ).astype(jnp.bfloat16)
    chosen = jnp.einsum(
        "sck,skw->scw",
        selector,
        every.reshape(shards, row_count, width),
        preferred_element_type=jnp.float32,
    ).astype(jnp.bfloat16)
    chosen = chosen.reshape(shards * CTX_DEV, width)
    pair_s = dot32(chosen, weights[:, 4 * HEAD_DIM :]).astype(jnp.bfloat16)
    student_mixed = attend(seed_queries, pair_s[:, :HEAD_DIM], pair_s[:, HEAD_DIM:])

    both = jnp.concatenate([target_mixed, student_mixed], axis=1)
    if rep == 1:
        both = both.reshape(shards, row_count, 2 * HEAD_DIM)
        both = lax.all_to_all(both, "seq", split_axis=0, concat_axis=0, tiled=True)
    else:
        both = lax.all_gather(both, "seq", axis=0, tiled=True)
        both = both.reshape(head_count, length, 2 * HEAD_DIM)
        both = lax.dynamic_slice_in_dim(both, me * row_count, row_count, axis=1)
    own_target = both[:, :, :HEAD_DIM].transpose(1, 0, 2).reshape(row_count, half_width)
    own_student = both[:, :, HEAD_DIM:].transpose(1, 0, 2).reshape(row_count, half_width)
    sums = jnp.concatenate(
        [
            dot32(own_target, target_out).astype(jnp.bfloat16),
            dot32(own_student, relaid).astype(jnp.bfloat16),
        ],
        axis=0,
    )
    if lax.axis_size("grp") == 2:
        other = lax.ppermute(sums, "grp", [(0, 1), (1, 0)])
        sums = sums.astype(jnp.float32) + other.astype(jnp.float32)
    else:
        sums = lax.psum(sums, "grp").astype(jnp.float32)

    features = layer_norm(tokens + sums[:row_count])[0].astype(jnp.bfloat16)
    own_seeds = lax.dynamic_slice_in_dim(seeds, me * row_count, row_count, axis=0)
    predicted, factor = layer_norm(own_seeds + sums[row_count:])
    places = me * row_count + jnp.arange(row_count, dtype=jnp.int32)
    usable = jnp.sum((lists[None, :] == places[:, None]).astype(jnp.float32), axis=1)
    slope = jnp.clip(predicted - features.astype(jnp.float32), -1.0, 1.0) * usable[:, None]
    back_grad = (
        slope
        - jnp.mean(slope, axis=1, keepdims=True)
        - predicted * jnp.mean(slope * predicted, axis=1, keepdims=True)
    ) * factor
    back_all = lax.all_gather(back_grad.astype(jnp.bfloat16), "seq", axis=0, tiled=True)
    head_grad = lax.dot_general(
        student_mixed,
        own_part(back_all),
        (((0,), (0,)), ((), ())),
        preferred_element_type=jnp.float32,
    ).astype(jnp.bfloat16)
    if lax.axis_size("dp") == 2:
        half = head_grad.shape[1] // 2
        first = lax.axis_index("dp") == 0
        low, high = head_grad[:, :half], head_grad[:, half:]
        keep, send = jnp.where(first, low, high), jnp.where(first, high, low)
        came = lax.ppermute(send, "dp", [(0, 1), (1, 0)])
        head_grad = (keep.astype(jnp.float32) + came.astype(jnp.float32)).astype(jnp.bfloat16)
    else:
        head_grad = lax.psum_scatter(head_grad, "dp", scatter_dimension=1, tiled=True)
    out_grad = lax.all_gather(head_grad, "seq", axis=0, tiled=True).astype(jnp.float32)
    if rep > 1:
        out_grad = out_grad.reshape(head_count, rep, HEAD_DIM, -1).sum(1)
        out_grad = out_grad.reshape(half_width, -1)
    target_blend = MOMENTUM * target_out.astype(jnp.float32) + (1.0 - MOMENTUM) * relaid.astype(
        jnp.float32
    )
    return (out_grad, target_blend)


def solution(mesh):
    in_specs = (
        P("dp", "seq", None),
        P("dp", "seq"),
        P("dp", "seq"),
        P(None, "dp", "grp"),
        P("grp", None),
        P(None, "dp", "grp"),
        P("grp", "dp"),
        P(),
    )
    out_specs = (P("grp", "dp"), P("grp", None))
    return jax.shard_map(body, mesh=mesh, in_specs=in_specs, out_specs=out_specs, check_vma=False)
```

time: 481 us -> 188 us (0.39)
  waiting for transfers between devices: 325 us -> 61.7 us
  local copies, waits for them, and re-layouts: 61.8 us -> 5.01 us
  other arithmetic: 14.7 us -> 31.1 us
  starting transfers between devices: 0.51 us -> 9.7 us
  blocking collectives: 38.6 us -> 47.2 us
  matrix products: 24.5 us -> 17.2 us
    all_gather x5 -> x2, waiting for transfers between devices: 224 us -> 35.6 us  [the longest x1 35.6 us: body(): lax.all_gather(back_grad.astype(jnp.bfloat16), 'seq', axis=0, tiled=True)]
    psum x2 -> x0, waiting for transfers between devices: 72 us -> none  [the longest x1 49.9 us: body(): out_grad = lax.psum(column_grad, 'seq').astype(jnp.float32)]
    unnamed x37, local copies, waits for them, and re-layouts: 43.8 us -> 2.71 us
    unnamed x9 -> x2, waiting for transfers between devices: 28.7 us -> 0.03 us
    unnamed x1, blocking collectives: 7.64 us -> 30.7 us
    ppermute x0 -> x4, waiting for transfers between devices: none -> 17.3 us  [the longest x1 16 us: body(): other = lax.ppermute(sums, 'grp', [(0, 1), (1, 0)])]
    all_gather x2 -> x1, blocking collectives: 31 us -> 16.5 us  [body(): lax.all_gather(head_grad, 'seq', axis=0, tiled=True).astype(jnp.float32)]
    slice x4 -> x3, local copies, waits for them, and re-layouts: 16.1 us -> 1.99 us  [the longest x1 1.97 us: body(): mine = jnp.concatenate([mine[k] for k in range(6)], axis=1)]
  transfers between devices with their start and end apart: 8 -> 7, of which waited for: 6 -> 4; matrix products, arithmetic and copies ran while one was open for 15% -> 19% of each run, Pallas kernels for 0% -> 0%
where the time goes in v1:
time: 188 us; the launch traced here: 187 us
  waiting for transfers between devices  61.7 us (33%)
  blocking collectives  47.2 us (25%)
  other arithmetic  31.1 us (17%)
  matrix products  17.2 us (9%)
  between operations  15.1 us (8%)
  starting transfers between devices  9.7 us (5%)
  local copies, waits for them, and re-layouts  5.01 us (3%)
    all_gather x1, waiting for transfers between devices, body(): lax.all_gather(back_grad.astype(jnp.bfloat16), 'seq', axis=0, tiled=True)  35.6 us
    unnamed x1, blocking collectives  30.7 us
    all_gather x1, blocking collectives, body(): lax.all_gather(head_grad, 'seq', axis=0, tiled=True).astype(jnp.float32)  16.5 us
    ppermute x1, waiting for transfers between devices, body(): other = lax.ppermute(sums, 'grp', [(0, 1), (1, 0)])  16 us
    all_to_all x1, waiting for transfers between devices, body(): both = lax.all_to_all(both, 'seq', split_axis=0, concat_axis=0, tiled=True)  8.81 us
    dot_general x4, matrix products, dot32(): return jnp.dot(left, right, preferred_element_type=jnp.float32)  5.82 us
    add x1, other arithmetic, body(): seeds = mask_token[None, :] + position_table(length, width)  5.49 us
    reduce_sum x3, other arithmetic, layer_norm(): jnp.mean(center * center, axis=-1, keepdims=True) + EPSILON  4.9 us
  transfers between devices with their start and end apart: 7, of which 4 were waited for; matrix products, arithmetic and copies ran while one was open for 19% of the time, Pallas kernels for 0%

profile of v1, /device:TPU:0, one launch (start us, length us, event | category | flops | bytes accessed | tf_op | source)
XLA Modules:
  0.0 187.0 jit_solution(831772082777444086)
XLA Ops:
  9.6 1.9 %fusion.23 = bf16[128,1408]{1,0:T(8,128)(2,1)} fusion(bf16[1,128,1408]{2,1,0:T(8,128)(2,1)} %param.8, f32[128]{0:T(128)S(1)} %add_rsqrt_fusion.3, f32[128]{0:T(128)S(1)} %broadcast_multiply_fusion.5), kind=kLoop, calls=%fused_computation.45 | loop fusion | flops 720896 | bytes 721920 | tf_op jit(solution)/shard_map/convert_element_type | solution.py:82
  11.6 2.0 %constant_dynamic-slice_fusion.4 = (bf16[1,704,88]{2,1,0:T(8,128)(2,1)S(1)}, bf16[1,704,88]{2,1,0:T(8,128)(2,1)S(1)}, bf16[1,704,88]{2,1,0:T(8,128)(2,1)S(1)}, b...) fusion(bf16[3,704,704]{2,1,0:T(8,128)(2,1)} %param.13, ...), kind=kLoop, calls=%fused_computation.103 | loop fusion | bytes 1486860 | tf_op jit(solution)/shard_map/slice | solution.py:78
  14.5 3.0 %collective-permute-start = (bf16[704,528]{0,1:T(8,128)(2,1)S(1)}, bf16[704,528]{0,1:T(8,128)(2,1)S(1)}, u32[]{:S(2)}, u32[]{:S(2)}) collective-permute-start(bf16[704,528]{0,1:T(8,128)(2,1)S(1)} %bitcast_dynamic-update-slice_fusion), channel_id=1, source_target_pairs={{0,1},{1,0},{2,3},{3,2},{4,5},{5,4},{6,7},{7,6},{8,9},{9,8},{10,11... | collective-permute-start | bytes 2230280 | tf_op jit(solution)/shard_map/ppermute | solution.py:53
  19.0 30.7 %all-reduce = s32[2560]{0:T(1024)S(1)} all-reduce(s32[2560]{0:T(1024)S(1)} %add_dynamic-update-slice_fusion), channel_id=2, replica_groups=mesh['seq'=8,'grp'=2,'dp'=2] {'seq'}, use_global_device_ids=true, to_apply=%add | all-reduce | flops 2560 | bytes 20480
  52.4 3.4 %multiply_reduce_fusion = (f32[32,32]{1,0:T(8,128)S(1)}, f32[32,32,1408]{2,1,0:T(8,128)}) fusion(f32[32,32]{1,0:T(8,128)S(1)} %broadcast_multiply_fusion, f32[1408]{0:T(1024)S(1)} %copy-done.8, f32[32,1408]{1,0:T(8,128)S(1)} %pad_maximum_fusion.8, f32[32,1408]{1,0:T(8,128)S(1)} %get-tuple-element.25, f32[32,1408]{1,0:T(8,128)S(1)} %get-tuple-element.40, ...), kind=kLoop, calls=%fused_computation.2 | loop fusion | flops 10091520 | bytes 6501888 | tf_op jit(solution)/shard_map/reduce_sum | solution.py:17
  55.9 5.5 %bitcast_add_fusion = f32[1024,1408]{1,0:T(8,128)} fusion(f32[32,32,1408]{2,1,0:T(8,128)} %get-tuple-element.21, f32[1408]{0:T(1024)S(1)} %copy-done.8), kind=kLoop, calls=%fused_computation | loop fusion | flops 1441792 | bytes 11539968 | tf_op jit(solution)/shard_map/add | solution.py:87
  61.6 2.9 %convolution_convert_fusion.4 = bf16[1024,264]{0,1:T(8,128)(2,1)S(1)} fusion(bf16[1024,1408]{1,0:T(8,128)(2,1)} %all-gather.4.cloned.1.call-done, bf16[704,528]{0,1:T(8,128)(2,1)S(1)} %get-tuple-element.18, bf16[704,528]{0,1:T(8,128)(2,1)S(1)} %get-tuple-element.17), kind=kOutput, calls=%fused_computation.21 | convolution fusion | flops 763023360 | bytes 4911104 | tf_op jit(solution)/shard_map/dot_general | solution.py:47
  68.1 4.1 %fusion.57 = (f32[1024]{0:T(1024)S(1)}, f32[1024,256]{0,1:T(8,128)S(1)}) fusion(bf16[256,176]{0,1:T(8,128)(2,1)S(1)} %convolution_convert_fusion.5, f32[1024,1408]{1,0:T(8,128)} %bitcast_add_fusion, f32[1024]{0:T(1024)S(1)} %rsqrt.36, f32[1024]{0:T(1024)S(1)} %div.51, bf16[704,528]{0,1:T(8,128)(2,1)S(1)} %get-tuple-element.18, ...), kind=kOutput, calls=%fused_computation.124 | convolution fusion | flops 305327104 | bytes 8495104 | tf_op jit(solution)/shard_map/dot_general | solution.py:37
  72.7 3.1 %fusion.11 = bf16[1024,88]{0,1:T(8,128)(2,1)S(1)} fusion(f32[1024,1024]{0,1:T(8,128)} %copy-done, f32[1024]{0:T(1024)S(1)} %get-tuple-element.35, bf16[1024,264]{0,1:T(8,128)(2,1)S(1)} %convolution_convert_fusion.4, f32[1024]{0:T(1024)S(1)} %fusion), kind=kOutput, calls=%fused_computation.25 | convolution fusion | flops 187875328 | bytes 4562944 | tf_op jit(solution)/shard_map/dot_general | solution.py:42
  76.6 3.4 %all-to-all-start = ((bf16[8,128,176]{1,2,0:T(8,128)(2,1)}), bf16[8,128,176]{1,2,0:T(8,128)(2,1)S(1)}, u32[]{:S(2)}, u32[]{:S(2)}) async-start(bf16[8,128,176]{1,2,0:T(8,128)(2,1)} %copy_bitcast_fusion), calls=%async_computation | async-start | bytes 720896 | tf_op jit(solution)/shard_map/all_to_all | solution.py:125
  80.3 2.7 %broadcast_select_fusion.1 = (bf16[704,704]{1,0:T(8,128)(2,1)S(1)}, bf16[704,704]{1,0:T(8,128)(2,1)}) fusion(bf16[704,704]{1,0:T(8,128)(2,1)} %param.14, bf16[704,704]{1,0:T(8,128)(2,1)} %collective-permute-done.1, pred[]{:T(512)S(6)} %eq.36), kind=kLoop, calls=%fused_computation.29 | loop fusion | flops 991232 | bytes 3964929 | tf_op jit(solution)/shard_map/jit(_where)/select_n | solution.py:56
  83.0 8.8 %all-to-all-done = bf16[8,128,176]{1,2,0:T(8,128)(2,1)S(1)} async-done(((bf16[8,128,176]{1,2,0:T(8,128)(2,1)}), bf16[8,128,176]{1,2,0:T(8,128)(2,1)S(1)}, u32[]{:S(2)}, u32[]{:S(2)}) %all-to-all-start) | async-done | bytes 360480 | tf_op jit(solution)/shard_map/all_to_all | solution.py:125
  92.4 2.0 %convolution_convert_fusion.1 = bf16[128,1408]{1,0:T(8,128)(2,1)S(1)} fusion(bf16[128,704]{0,1:T(8,128)(2,1)S(1)} %bitcast.62, bf16[704,704]{1,0:T(8,128)(2,1)} %get-tuple-element.16, bf16[704,704]{1,0:T(8,128)(2,1)S(1)} %get-tuple-element.15), kind=kOutput, calls=%fused_computation.14 | convolution fusion | flops 257900544 | bytes 2523136 | tf_op jit(solution)/shard_map/dot_general | solution.py:47
  95.4 1.4 collective-permute-start.2
  97.1 16.0 %collective-permute-done.2 = bf16[256,1408]{1,0:T(8,128)(2,1)} collective-permute-done((bf16[256,1408]{1,0:T(8,128)(2,1)}, bf16[256,1408]{1,0:T(8,128)(2,1)}, u32[]{:S(2)}, u32[]{:S(2)}) %collective-permute-start.2) | collective-permute-done | bytes 720928 | tf_op jit(solution)/shard_map/ppermute | solution.py:140
  113.1 1.5 convert_add_fusion
  114.7 1.4 fusion.54
  118.0 35.6 %all-gather.6.cloned.1.call-done = bf16[1024,1408]{1,0:T(8,128)(2,1)} async-done(((bf16[128,1408]{1,0:T(8,128)(2,1)}), bf16[1024,1408]{1,0:T(8,128)(2,1)}) %all-gather.6.cloned.1.call-update) | async-done | bytes 2883600 | tf_op jit(solution)/shard_map/all_gather | solution.py:156
  153.6 2.6 %convolution_convert_fusion.3 = bf16[88,1408]{1,0:T(8,128)(2,1)S(1)} fusion(bf16[1024,88]{0,1:T(8,128)(2,1)} %copy-done.7, bf16[1024,1408]{1,0:T(8,128)(2,1)} %all-gather.6.cloned.1.call-done), kind=kOutput, calls=%fused_computation.16 | convolution fusion | flops 253879296 | bytes 3311616 | tf_op jit(solution)/shard_map/dot_general | solution.py:157
  156.3 1.5 collective-permute-start.3
  157.8 3.0 %multiply_add_fusion.1 = f32[704,1408]{1,0:T(8,128)} fusion(bf16[704,1408]{1,0:T(8,128)(2,1)S(1)} %copy-done.2, bf16[704,704]{1,0:T(8,128)(2,1)S(1)} %copy-done.3, bf16[704,704]{1,0:T(8,128)(2,1)S(1)} %get-tuple-element.15), kind=kLoop, calls=%fused_computation.6 | loop fusion | flops 7929856 | bytes 7929856 | tf_op jit(solution)/shard_map/add | solution.py:176
  160.8 1.2 collective-permute-done.3
  162.2 16.5 %all_gather.19 = bf16[704,704]{1,0:T(8,128)(2,1)S(1)} all-gather(bf16[88,704]{1,0:T(8,128)(2,1)S(1)} %add_convert_fusion), channel_id=1, replica_groups=mesh['seq'=8,'grp'=2,'dp'=2] {'seq'}, dimensions={0}, use_global_device_ids=true | all-gather | bytes 1115136 | tf_op jit(solution)/shard_map/all_gather | solution.py:172
  178.7 1.5 convert_element_type.138
  (93 shorter events, 16.1 us)
Async XLA Ops:
  7.2 10.5 %copy-start.11 = (u32[32]{0:T(128)S(1)}, u32[32]{0:T(128)}, u32[]{:S(2)}) copy-start(u32[32]{0:T(128)} %constant.78) | copy-start | bytes 388
  7.2 11.7 %copy-start.10 = (s32[1,128]{1,0:T(1,128)S(1)}, s32[1,128]{1,0:T(1,128)}, u32[]{:S(2)}) copy-start(s32[1,128]{1,0:T(1,128)} %param.9) | copy-start | bytes 1540
  7.2 11.7 %copy-start.9 = (s32[1,192]{1,0:T(1,128)S(1)}, s32[1,192]{1,0:T(1,128)}, u32[]{:S(2)}) copy-start(s32[1,192]{1,0:T(1,128)} %param.10) | copy-start | bytes 2308
  7.2 54.3 %all-gather.4.cloned.1.call-start = ((), (), s32[]{:S(2)}) async-start(), calls=%async_computation.1 | async-start | bytes 3244032 | tf_op jit(solution)/shard_map/all_gather | solution.py:83
  11.6 39.6 %copy-start.8 = (f32[1408]{0:T(1024)S(1)}, f32[1408]{0:T(1024)}, u32[]{:S(2)}) copy-start(f32[1408]{0:T(1024)} %param.15) | copy-start | bytes 16900
  14.5 46.9 %collective-permute-start = (bf16[704,528]{0,1:T(8,128)(2,1)S(1)}, bf16[704,528]{0,1:T(8,128)(2,1)S(1)}, u32[]{:S(2)}, u32[]{:S(2)}) collective-permute-start(bf16[704,528]{0,1:T(8,128)(2,1)S(1)} %bitcast_dynamic-update-slice_fusion), channel_id=1, source_target_pairs={{0,1},{1,0},{2,3},{3,2},{4,5},{5,4},{6,7},{7,6},{8,9},{9,8},{10,11... | collective-permute-start | bytes 2230280 | tf_op jit(solution)/shard_map/ppermute | solution.py:53
  17.6 62.7 %collective-permute-start.1 = (bf16[704,704]{1,0:T(8,128)(2,1)}, bf16[704,704]{1,0:T(8,128)(2,1)}, u32[]{:S(2)}, u32[]{:S(2)}) collective-permute-start(bf16[704,704]{1,0:T(8,128)(2,1)} %param.14), channel_id=1, source_target_pairs={{0,1},{1,0},{2,3},{3,2},{4,5},{5,4},{6,7},{7,6},{8,9},{9,8},{10,11... | collective-permute-start | bytes 2973704 | tf_op jit(solution)/shard_map/ppermute | solution.py:53
  64.4 2.0 %copy-start.5 = (bf16[1024,1408]{1,0:T(8,128)(2,1)S(1)}, bf16[1024,1408]{1,0:T(8,128)(2,1)}, u32[]{:S(2)}) copy-start(bf16[1024,1408]{1,0:T(8,128)(2,1)} %all-gather.4.cloned.1.call-done) | copy-start | bytes 8650756
  65.2 2.1 %copy-start = (f32[1024,1024]{0,1:T(8,128)}, f32[1024,1024]{0,1:T(8,128)S(1)}, u32[]{:S(2)}) copy-start(f32[1024,1024]{0,1:T(8,128)S(1)} %get-tuple-element.36) | copy-start | bytes 12582916
  72.7 3.1 %copy-start.7 = (bf16[1024,88]{0,1:T(8,128)(2,1)}, bf16[1024,88]{0,1:T(8,128)(2,1)S(1)}, u32[]{:S(2)}) copy-start(bf16[1024,88]{0,1:T(8,128)(2,1)S(1)} %fusion.10) | copy-start | bytes 540676
  75.8 16.0 %copy-start.2 = (bf16[704,1408]{1,0:T(8,128)(2,1)S(1)}, bf16[704,1408]{1,0:T(8,128)(2,1)}, u32[]{:S(2)}) copy-start(bf16[704,1408]{1,0:T(8,128)(2,1)} %param.12) | copy-start | bytes 5947396
  76.6 15.2 %all-to-all-start = ((bf16[8,128,176]{1,2,0:T(8,128)(2,1)}), bf16[8,128,176]{1,2,0:T(8,128)(2,1)S(1)}, u32[]{:S(2)}, u32[]{:S(2)}) async-start(bf16[8,128,176]{1,2,0:T(8,128)(2,1)} %copy_bitcast_fusion), calls=%async_computation | async-start | bytes 720896 | tf_op jit(solution)/shard_map/all_to_all | solution.py:125
  80.0 73.5 %all-gather.6.cloned.1.call-start = ((), (), s32[]{:S(2)}) async-start(), calls=%async_computation.2 | async-start | bytes 3244032 | tf_op jit(solution)/shard_map/all_gather | solution.py:156
  92.3 2.1 %copy-start.4 = (bf16[128,1408]{1,0:T(8,128)(2,1)}, bf16[128,1408]{1,0:T(8,128)(2,1)S(1)}, u32[]{:S(2)}) copy-start(bf16[128,1408]{1,0:T(8,128)(2,1)S(1)} %convolution_convert_fusion.2) | copy-start | bytes 1081348
  92.3 22.2 %copy-start.1 = (bf16[1,128,1408]{2,1,0:T(8,128)(2,1)S(1)}, bf16[1,128,1408]{2,1,0:T(8,128)(2,1)}, u32[]{:S(2)}) copy-start(bf16[1,128,1408]{2,1,0:T(8,128)(2,1)} %param.8) | copy-start | bytes 1081348
  94.4 1.0 copy-start.6
  95.4 17.7 %collective-permute-start.2 = (bf16[256,1408]{1,0:T(8,128)(2,1)}, bf16[256,1408]{1,0:T(8,128)(2,1)}, u32[]{:S(2)}, u32[]{:S(2)}) collective-permute-start(bf16[256,1408]{1,0:T(8,128)(2,1)} %pad_maximum_fusion.4), channel_id=1, source_target_pairs={{0,2},{2,0},{1,3},{3,1},{4,6},{6,4},{5,7},{7,5},{8,10},{10,8},{9,1... | collective-permute-start | bytes 2162696 | tf_op jit(solution)/shard_map/ppermute | solution.py:140
  153.6 4.3 %copy-start.3 = (bf16[704,704]{1,0:T(8,128)(2,1)S(1)}, bf16[704,704]{1,0:T(8,128)(2,1)}, u32[]{:S(2)}) copy-start(bf16[704,704]{1,0:T(8,128)(2,1)} %get-tuple-element.16) | copy-start | bytes 2973700
  156.3 5.8 %collective-permute-start.3 = (bf16[88,704]{1,0:T(8,128)(2,1)S(1)}, bf16[88,704]{1,0:T(8,128)(2,1)S(1)}, u32[]{:S(2)}, u32[]{:S(2)}) collective-permute-start(bf16[88,704]{1,0:T(8,128)(2,1)S(1)} %broadcast_select_fusion.4), channel_id=1, source_target_pairs={{0,1},{1,0},{2,3},{3,2},{4,5},{5,4},{6,7},{7,6},{8,9},{9,8},{10,11... | collective-permute-start | bytes 371720 | tf_op jit(solution)/shard_map/ppermute | solution.py:168
Sparse Core Ops, SparseCore 0:
  11.7 39.2 all-gather.3
  118.1 35.4 all-gather.5

commit v2 on v1

--- a/solution.py
+++ b/solution.py
@@ -1,9 +1,15 @@
+import functools
 import math
 
 import jax
 import jax.numpy as jnp
 from jax import lax
+from jax.experimental import pallas as pl
+from jax.experimental.pallas import tpu as pltpu
 from jax.sharding import PartitionSpec as P
+
+MESH = pl.DeviceIdType.MESH
+CHUNKS = 2
 
 HEAD_DIM = 88
 CTX_DEV = 32
@@ -18,19 +24,232 @@
     return (center * factor, factor)
 
 
-def position_table(length, width):
+def position_tables(length, width):
     half_width = width // 2
     spacing = jnp.exp(jnp.arange(half_width, dtype=jnp.float32) * (-math.log(10000.0) / half_width))
     high = (jnp.arange(length // STRIDE) * STRIDE).astype(jnp.float32)[:, None] * spacing[None, :]
     low = jnp.arange(STRIDE).astype(jnp.float32)[:, None] * spacing[None, :]
     sin_h, cos_h = jnp.sin(high), jnp.cos(high)
     sin_l, cos_l = jnp.sin(low), jnp.cos(low)
-    first = jnp.concatenate([sin_h, cos_h], axis=1)
-    second = jnp.concatenate([cos_h, -sin_h], axis=1)
-    twice_c = jnp.concatenate([cos_l, cos_l], axis=1)
-    twice_s = jnp.concatenate([sin_l, sin_l], axis=1)
-    table = first[:, None, :] * twice_c[None] + second[:, None, :] * twice_s[None]
-    return table.reshape(length, width)
+    return (
+        jnp.concatenate([sin_h, cos_h], axis=1),
+        jnp.concatenate([cos_h, -sin_h], axis=1),
+        jnp.concatenate([cos_l, cos_l], axis=1),
+        jnp.concatenate([sin_l, sin_l], axis=1),
+    )
+
+
+def norm_seed_block(index, tables, mask_ref, seed_out):
+    first, second, twice_c, twice_s = tables
+    rows = pl.ds(index, 1)
+    seeds = mask_ref[...] + (first[rows, :] * twice_c[...] + second[rows, :] * twice_s[...])
+    start = pl.multiple_of(index * STRIDE, STRIDE)
+    seed_out[pl.ds(start, STRIDE), :] = layer_norm(seeds)[0].astype(jnp.bfloat16)
+
+
+def gather_kernel(shards, with_seeds, *refs):
+    if with_seeds:
+        (x_ref, small_ref, *tables, mask_ref, out_ref, small_out, seed_out) = refs[:10]
+        sems = refs[10:]
+        s_send, s_recv, s_own = sems[7:]
+    else:
+        x_ref, out_ref = refs[:2]
+        sems = refs[2:]
+    own_sem, z_send, z_recv, m_send, m_recv, y_send, y_recv = sems[:7]
+    me, grp = lax.axis_index("seq"), lax.axis_index("grp")
+    z, core = me // 2, me % 2
+    depth = shards // 2
+    mate, across = z * 2 + (1 - core), 1 - grp
+    pieces = range(CHUNKS)
+
+    barrier = pltpu.get_barrier_semaphore()
+    if with_seeds:
+        for k in range(1, shards):
+            peer = {"seq": lax.rem(me + k, shards)}
+            pl.semaphore_signal(barrier, inc=1, device_id=peer, device_id_type=MESH)
+        greeted = shards - 1
+    else:
+        for k in range(1, depth):
+            peer = {"seq": lax.rem(z + k, depth) * 2 + core}
+            pl.semaphore_signal(barrier, inc=1, device_id=peer, device_id_type=MESH)
+        pl.semaphore_signal(barrier, inc=1, device_id={"seq": mate}, device_id_type=MESH)
+        greeted = depth
+    pl.semaphore_signal(barrier, inc=1, device_id={"grp": across}, device_id_type=MESH)
+    pl.semaphore_wait(barrier, greeted + 1)
+
+    def remote(src, slot, group, piece, send, recv, to):
+        return pltpu.make_async_remote_copy(
+            src_ref=src,
+            dst_ref=out_ref.at[slot, group, piece],
+            send_sem=send,
+            recv_sem=recv,
+            device_id=to,
+            device_id_type=MESH,
+        )
+
+    def z_copy(way, dist, piece):
+        sign = 1 - 2 * way
+        to = {"seq": (z + sign * dist) * 2 + core}
+        return remote(
+            x_ref.at[piece], me, grp, piece,
+            z_send.at[way, dist - 1, piece], z_recv.at[way, dist - 1, piece], to,
+        )
+
+    def goes(way, dist):
+        return z + dist < depth if way == 0 else z - dist >= 0
+
+    def comes(way, dist):
+        return goes(1 - way, dist)
+
+    def mate_copy(src, source, side, piece):
+        group = grp if side == 0 else across
+        return remote(
+            src, source * 2 + core, group, piece,
+            m_send.at[side, source, piece], m_recv.at[side, source, piece], {"seq": mate},
+        )
+
+    def y_copy(src, source, piece):
+        return remote(
+            src, source * 2 + core, grp, piece,
+            y_send.at[source, piece], y_recv.at[source, piece], {"grp": across},
+        )
+
+    def small_copy(k):
+        return pltpu.make_async_remote_copy(
+            src_ref=small_ref,
+            dst_ref=small_out.at[me],
+            send_sem=s_send.at[k - 1],
+            recv_sem=s_recv.at[k - 1],
+            device_id={"seq": lax.rem(me + k, shards)},
+            device_id_type=MESH,
+        )
+
+    for dist in range(1, depth):
+        for way in range(2):
+
+            @pl.when(goes(way, dist))
+            def _():
+                for piece in pieces:
+                    z_copy(way, dist, piece).start()
+
+    for piece in pieces:
+        y_copy(x_ref.at[piece], z, piece).start()
+        mate_copy(x_ref.at[piece], z, 0, piece).start()
+    own = pltpu.make_async_copy(x_ref, out_ref.at[me, grp], own_sem)
+    own.start()
+    if with_seeds:
+        for k in range(1, shards):
+            small_copy(k).start()
+        small_own = pltpu.make_async_copy(small_ref, small_out.at[me], s_own)
+        small_own.start()
+        blocks = seed_out.shape[0] // STRIDE
+        stages = depth + 1
+
+    def work(stage):
+        if with_seeds:
+            lax.fori_loop(
+                stage * blocks // stages,
+                (stage + 1) * blocks // stages,
+                lambda i, _: (norm_seed_block(i, tables, mask_ref, seed_out), 0)[1],
+                0,
+            )
+
+    def from_z(way, dist):
+        source = z - dist if way == 0 else z + dist
+
+        @pl.when(comes(way, dist))
+        def _():
+            for piece in pieces:
+                z_copy(way, dist, piece).wait_recv()
+                held = out_ref.at[source * 2 + core, grp, piece]
+                y_copy(held, source, piece).start()
+                mate_copy(held, source, 0, piece).start()
+
+    def from_y(source):
+        for piece in pieces:
+            held = out_ref.at[source * 2 + core, across, piece]
+            y_copy(held, source, piece).wait_recv()
+            mate_copy(held, source, 1, piece).start()
+
+    work(0)
+    from_y(z)
+    for dist in range(1, depth):
+        work(dist)
+        for way in range(2):
+            from_z(way, dist)
+        if dist > 1:
+            for way in range(2):
+
+                @pl.when(comes(way, dist - 1))
+                def _():
+                    from_y(z - (dist - 1) if way == 0 else z + (dist - 1))
+
+    work(depth)
+    for way in range(2):
+
+        @pl.when(comes(way, depth - 1))
+        def _():
+            from_y(z - (depth - 1) if way == 0 else z + (depth - 1))
+
+    for source in range(depth):
+        for piece in pieces:
+            for side in range(2):
+                mate_copy(out_ref.at[source * 2 + core, grp, piece], source, side, piece).wait()
+            y_copy(out_ref.at[source * 2 + core, grp, piece], source, piece).wait_send()
+    for dist in range(1, depth):
+        for way in range(2):
+
+            @pl.when(goes(way, dist))
+            def _():
+                for piece in pieces:
+                    z_copy(way, dist, piece).wait_send()
+
+    own.wait()
+    if with_seeds:
+        for k in range(1, shards):
+            small_copy(k).wait()
+        small_own.wait()
+
+
+def gather_rows(rows, shards, small=None, tables=None, mask=None):
+    count, width = rows.shape
+    depth = shards // 2
+    dma = pltpu.SemaphoreType.DMA
+    shaped = rows.reshape(CHUNKS, count // CHUNKS, width)
+    out_shape = [jax.ShapeDtypeStruct((shards, 2) + shaped.shape, rows.dtype)]
+    operands = [shaped]
+    scratch = [
+        dma,
+        dma((2, depth - 1, CHUNKS)),
+        dma((2, depth - 1, CHUNKS)),
+        dma((2, depth, CHUNKS)),
+        dma((2, depth, CHUNKS)),
+        dma((depth, CHUNKS)),
+        dma((depth, CHUNKS)),
+    ]
+    with_seeds = small is not None
+    if with_seeds:
+        operands += [small, *tables, mask[None, :]]
+        out_shape += [
+            jax.ShapeDtypeStruct((shards,) + small.shape, small.dtype),
+            jax.ShapeDtypeStruct((tables[0].shape[0] * STRIDE, width), jnp.bfloat16),
+        ]
+        scratch += [dma((shards - 1,)), dma((shards - 1,)), dma]
+    vmem = pl.BlockSpec(memory_space=pltpu.VMEM)
+    results = pl.pallas_call(
+        functools.partial(gather_kernel, shards, with_seeds),
+        out_shape=out_shape,
+        in_specs=[vmem] * len(operands),
+        out_specs=[vmem] * len(out_shape),
+        scratch_shapes=scratch,
+        name="gather_seeds" if with_seeds else "gather_rows",
+        compiler_params=pltpu.CompilerParams(
+            collective_id=1 if with_seeds else 2,
+            has_side_effects=True,
+            vmem_limit_bytes=48 * 1024 * 1024,
+        ),
+    )(*operands)
+    return (results[0].reshape(shards * 2 * count, width), *results[1:])
 
 
 def attend(queries, keys, values):
@@ -60,8 +279,7 @@
 def body(
     clips, context, predict_index, target_qkv, target_out, student_qkv, student_out, mask_token
 ):
-    tokens = clips[0].astype(jnp.float32)
-    row_count, width = tokens.shape
+    row_count, width = clips.shape[1:]
     half_width = target_qkv.shape[2]
     head_count = half_width // HEAD_DIM
     shards = lax.axis_size("seq")
@@ -79,13 +297,18 @@
     weights = both_of_dp(mine, 0)
     relaid = both_of_dp(student_out, 1)
 
-    normed = layer_norm(tokens)[0].astype(jnp.bfloat16)
-    every = lax.all_gather(normed, "seq", axis=0, tiled=True)
-    small = lax.all_gather(jnp.concatenate([context[0], predict_index[0]]), "seq", axis=0)
-    flags, lists = small[:, :row_count], small[:, row_count:].reshape(-1)
-
-    seeds = mask_token[None, :] + position_table(length, width)
-    seed_normed = layer_norm(seeds)[0].astype(jnp.bfloat16)
+    grp = lax.axis_index("grp")
+    half_rows = row_count // 2
+    own_tokens = lax.dynamic_slice_in_dim(clips[0], grp * half_rows, half_rows, axis=0)
+    own_tokens = own_tokens.astype(jnp.float32)
+    normed = layer_norm(own_tokens)[0].astype(jnp.bfloat16)
+    tables = position_tables(length, width)
+    small = jnp.concatenate([context[0], predict_index[0]])[None, :]
+    small = jnp.pad(small, ((0, 7), (0, -small.shape[1] % 128)))
+    every, small, seed_normed = gather_rows(normed, shards, small, tables, mask_token)
+    small = small[:, 0]
+    flags = small[:, :row_count]
+    lists = small[:, row_count : row_count + predict_index.shape[1]].reshape(-1)
 
     def own_part(rows):
         if rep == 1:
@@ -129,23 +352,27 @@
         both = lax.dynamic_slice_in_dim(both, me * row_count, row_count, axis=1)
     own_target = both[:, :, :HEAD_DIM].transpose(1, 0, 2).reshape(row_count, half_width)
     own_student = both[:, :, HEAD_DIM:].transpose(1, 0, 2).reshape(row_count, half_width)
-    sums = jnp.concatenate(
+    sums = jnp.stack(
         [
             dot32(own_target, target_out).astype(jnp.bfloat16),
             dot32(own_student, relaid).astype(jnp.bfloat16),
-        ],
-        axis=0,
+        ]
     )
-    if lax.axis_size("grp") == 2:
-        other = lax.ppermute(sums, "grp", [(0, 1), (1, 0)])
-        sums = sums.astype(jnp.float32) + other.astype(jnp.float32)
-    else:
-        sums = lax.psum(sums, "grp").astype(jnp.float32)
-
-    features = layer_norm(tokens + sums[:row_count])[0].astype(jnp.bfloat16)
-    own_seeds = lax.dynamic_slice_in_dim(seeds, me * row_count, row_count, axis=0)
-    predicted, factor = layer_norm(own_seeds + sums[row_count:])
-    places = me * row_count + jnp.arange(row_count, dtype=jnp.int32)
+    low, high = sums[:, :half_rows], sums[:, half_rows:]
+    keep, send = jnp.where(grp == 0, low, high), jnp.where(grp == 0, high, low)
+    came = lax.ppermute(send, "grp", [(0, 1), (1, 0)])
+    sums = keep.astype(jnp.float32) + came.astype(jnp.float32)
+
+    features = layer_norm(own_tokens + sums[0])[0].astype(jnp.bfloat16)
+    base = me * row_count + grp * half_rows
+    first, second, twice_c, twice_s = tables
+    blocks = half_rows // STRIDE
+    first = lax.dynamic_slice_in_dim(first, base // STRIDE, blocks, axis=0)
+    second = lax.dynamic_slice_in_dim(second, base // STRIDE, blocks, axis=0)
+    own_seeds = first[:, None] * twice_c[None] + second[:, None] * twice_s[None]
+    own_seeds = mask_token[None, :] + own_seeds.reshape(half_rows, width)
+    predicted, factor = layer_norm(own_seeds + sums[1])
+    places = base + jnp.arange(half_rows, dtype=jnp.int32)
     usable = jnp.sum((lists[None, :] == places[:, None]).astype(jnp.float32), axis=1)
     slope = jnp.clip(predicted - features.astype(jnp.float32), -1.0, 1.0) * usable[:, None]
     back_grad = (
@@ -153,7 +380,7 @@
         - jnp.mean(slope, axis=1, keepdims=True)
         - predicted * jnp.mean(slope * predicted, axis=1, keepdims=True)
     ) * factor
-    back_all = lax.all_gather(back_grad.astype(jnp.bfloat16), "seq", axis=0, tiled=True)
+    back_all = gather_rows(back_grad.astype(jnp.bfloat16), shards)[0]
     head_grad = lax.dot_general(
         student_mixed,
         own_part(back_all),

time: 188 us -> 151 us (0.80)
  Pallas kernels: 0 us -> 59.4 us
  waiting for transfers between devices: 61.7 us -> 17.8 us
  blocking collectives: 47.2 us -> 16.2 us
  between operations: 15.1 us -> 1.17 us
  other arithmetic: 31.1 us -> 22.1 us
  local copies, waits for them, and re-layouts: 5.01 us -> 11.8 us
  matrix products: 17.2 us -> 13 us
    pallas_call x0 -> x2, Pallas kernels: none -> 59.4 us  [gather_rows(): pl.pallas_call(functools.partial(gather_kernel, shards, with_seeds), out_...]
    all_gather x2 -> x0, waiting for transfers between devices: 35.6 us -> none  [the longest x1 35.6 us: body(): lax.all_gather(back_grad.astype(jnp.bfloat16), 'seq', axis=0, tiled=True)]
    unnamed x1 -> x0, blocking collectives: 30.7 us -> none
    ppermute x1, waiting for transfers between devices: 16 us -> 9.1 us  [body(): came = lax.ppermute(send, 'grp', [(0, 1), (1, 0)])]
    add x3, other arithmetic: 6.95 us -> 0.7 us  [the longest x1 0.54 us: body(): places = base + jnp.arange(half_rows, dtype=jnp.int32)]
    reduce_sum x3, other arithmetic: 4.9 us -> 1.62 us  [layer_norm(): jnp.mean(center * center, axis=-1, keepdims=True) + EPSILON]
    reduce_sum x4 -> x2, other arithmetic: 3.87 us -> 1.03 us  [layer_norm(): center = values - jnp.mean(values, axis=-1, keepdims=True)]
    dot_general x4, matrix products: 5.82 us -> 3.37 us  [dot32(): return jnp.dot(left, right, preferred_element_type=jnp.float32)]
  transfers between devices with their start and end apart: 7 -> 5, of which waited for: 4 -> 3; matrix products, arithmetic and copies ran while one was open for 19% -> 19% of each run, Pallas kernels for 0% -> 23%
where the time goes in v2:
time: 151 us
  Pallas kernels  59.4 us (39%)
  other arithmetic  22.1 us (15%)
  waiting for transfers between devices  17.8 us (12%)
  blocking collectives  16.2 us (11%)
  matrix products  13 us (9%)
  local copies, waits for them, and re-layouts  11.8 us (8%)
  starting transfers between devices  9.5 us (6%)
    pallas_call x2, Pallas kernels, gather_rows(): pl.pallas_call(functools.partial(gather_kernel, shards, with_seeds), out_...  59.4 us
    all_gather x1, blocking collectives, body(): lax.all_gather(head_grad, 'seq', axis=0, tiled=True).astype(jnp.float32)  16.2 us
    ppermute x1, waiting for transfers between devices, body(): came = lax.ppermute(send, 'grp', [(0, 1), (1, 0)])  9.1 us
    all_to_all x1, waiting for transfers between devices, body(): both = lax.all_to_all(both, 'seq', split_axis=0, concat_axis=0, tiled=True)  7.37 us
    dot_general x2, matrix products, attend(): lax.dot_general(queries, keys, (((1,), (1,)), ((), ())), preferred_elemen...  5.81 us
    all_to_all x1, starting transfers between devices, body(): both = lax.all_to_all(both, 'seq', split_axis=0, concat_axis=0, tiled=True)  4.4 us
    unnamed x58, local copies, waits for them, and re-layouts  4.33 us
    select_n x2, other arithmetic, both_of_dp(): jnp.where(first, block, other)  4.18 us
  transfers between devices with their start and end apart: 5, of which 3 were waited for; matrix products, arithmetic and copies ran while one was open for 19% of the time, Pallas kernels for 23%

profile of v2, /device:TPU:0, one launch (start us, length us, event | category | flops | bytes accessed | tf_op | source)
XLA Modules:
  0.0 150.9 jit_solution(9486428823201253627)
XLA Ops:
  0.7 2.0 %constant_dynamic-slice_fusion.4 = (bf16[1,704,88]{2,1,0:T(8,128)(2,1)S(1)}, bf16[1,704,88]{2,1,0:T(8,128)(2,1)S(1)}, bf16[1,704,88]{2,1,0:T(8,128)(2,1)S(1)}, b...) fusion(bf16[3,704,704]{2,1,0:T(8,128)(2,1)} %param.13, ...), kind=kLoop, calls=%fused_computation.105 | loop fusion | bytes 1486860 | tf_op jit(solution)/shard_map/slice | solution.py:296
  7.5 3.0 %collective-permute-start = (bf16[704,528]{0,1:T(8,128)(2,1)}, bf16[704,528]{0,1:T(8,128)(2,1)}, u32[]{:S(2)}, u32[]{:S(2)}) collective-permute-start(bf16[704,528]{0,1:T(8,128)(2,1)} %bitcast_dynamic-update-slice_fusion), channel_id=1, source_target_pairs={{0,1},{1,0},{2,3},{3,2},{4,5},{5,4},{6,7},{7,6},{8,9},{9,8},{10,11... | collective-permute-start | bytes 2230280 | tf_op jit(solution)/shard_map/ppermute | solution.py:272
  12.3 34.1 %gather_seeds.1 = (bf16[8,2,2,32,1408]{4,3,2,1,0:T(8,128)(2,1)S(1)}, s32[8,8,384]{2,1,0:T(8,128)S(1)}, bf16[1024,1408]{1,0:T(8,128)(2,1)}) custom-call(bf16[2,32,1408]{2,1,0:T(8,128)(2,1)S(1)} %multiply_convert_fusion.3.refs_0_, s32[8,384]{1,0:T(8,128)S(1)} %pad.4.refs_1_, f32[32,1408]{1,0:T(8,128)S(1)} %get-tuple-element.32.refs_2_, ...), custom_call_target="tpu_custom_call" | custom-call | tf_op jit(solution)/shard_map/gather_seeds/pallas_call | solution.py:239
  49.1 1.1 convolution_convert_fusion
  50.3 1.5 broadcast_select_fusion.3
  51.8 1.1 convolution_convert_fusion.6
  54.1 2.7 %multiply_reduce_fusion = (f32[1024]{0:T(1024)S(1)}, f32[1024,1024]{0,1:T(8,128)}) fusion(bf16[1024,264]{0,1:T(8,128)(2,1)S(1)} %convolution_convert_fusion.4), kind=kOutput, calls=%fused_computation.2 | convolution fusion | flops 186645504 | bytes 4558848 | tf_op jit(solution)/shard_map/dot_general | solution.py:256
  56.8 3.1 %fusion.55 = (f32[1024]{0:T(1024)S(1)}, f32[1024,256]{0,1:T(8,128)S(1)}) fusion(bf16[256,176]{0,1:T(8,128)(2,1)S(1)} %copy-done.15, bf16[1024,1408]{1,0:T(8,128)(2,1)} %get-tuple-element.5, bf16[704,528]{0,1:T(8,128)(2,1)} %copy-done.3, bf16[704,528]{0,1:T(8,128)(2,1)} %copy-done.2), kind=kOutput, calls=%fused_computation.129 | convolution fusion | flops 301001728 | bytes 5468160 | tf_op jit(solution)/shard_map/dot_general | solution.py:256
  60.1 3.1 %fusion = f32[1024]{0:T(1024)S(1)} fusion(f32[1024,1024]{0,1:T(8,128)} %get-tuple-element.44, f32[1024]{0:T(1024)S(1)} %get-tuple-element.43), kind=kLoop, calls=%fused_computation.3 | loop fusion | flops 3144704 | bytes 4202496 | tf_op jit(solution)/shard_map/reduce_sum | solution.py:260
  63.5 1.8 %fusion.10 = bf16[1024,88]{0,1:T(8,128)(2,1)S(1)} fusion(f32[1024,1024]{0,1:T(8,128)S(1)} %copy-done, f32[1024]{0:T(1024)S(1)} %get-tuple-element.43, bf16[1024,264]{0,1:T(8,128)(2,1)} %copy-done.14, f32[1024]{0:T(1024)S(1)} %fusion), kind=kOutput, calls=%fused_computation.18 | convolution fusion | flops 187875328 | bytes 4562944 | tf_op jit(solution)/shard_map/dot_general | solution.py:261
  66.1 4.4 %all-to-all-start = ((bf16[8,128,176]{1,2,0:T(8,128)(2,1)}), bf16[8,128,176]{1,2,0:T(8,128)(2,1)}, u32[]{:S(2)}, u32[]{:S(2)}) async-start(bf16[8,128,176]{1,2,0:T(8,128)(2,1)} %copy_bitcast_fusion), calls=%async_computation | async-start | bytes 720896 | tf_op jit(solution)/shard_map/all_to_all | solution.py:348
  72.1 2.7 %broadcast_select_fusion.1 = (bf16[704,704]{1,0:T(8,128)(2,1)S(1)}, bf16[704,704]{1,0:T(8,128)(2,1)}) fusion(bf16[704,704]{1,0:T(8,128)(2,1)} %param.14, bf16[704,704]{1,0:T(8,128)(2,1)} %collective-permute-done.1, pred[]{:T(512)S(6)} %eq.40), kind=kLoop, calls=%fused_computation.22 | loop fusion | flops 991232 | bytes 3964929 | tf_op jit(solution)/shard_map/jit(_where)/select_n | solution.py:275
  74.8 7.4 %all-to-all-done = bf16[8,128,176]{1,2,0:T(8,128)(2,1)} async-done(((bf16[8,128,176]{1,2,0:T(8,128)(2,1)}), bf16[8,128,176]{1,2,0:T(8,128)(2,1)}, u32[]{:S(2)}, u32[]{:S(2)}) %all-to-all-start) | async-done | bytes 360480 | tf_op jit(solution)/shard_map/all_to_all | solution.py:348
  82.2 1.1 fusion.54
  85.3 9.1 %collective-permute-done.2 = bf16[2,64,1408]{2,1,0:T(8,128)(2,1)S(1)} collective-permute-done((bf16[2,64,1408]{2,1,0:T(8,128)(2,1)S(1)}, bf16[2,64,1408]{2,1,0:T(8,128)(2,1)S(1)}, u32[]{:S(2)}, u32[]{:S(2)}) %collective-permute-start.2) | collective-permute-done | bytes 360480 | tf_op jit(solution)/shard_map/ppermute | solution.py:363
  96.6 1.2 multiply_reduce_fusion.3
  97.9 1.3 fusion.24
  99.6 1.5 multiply_convert_fusion.refs_0_
  101.1 25.3 %gather_rows.1 = bf16[8,2,2,32,1408]{4,3,2,1,0:T(8,128)(2,1)S(1)} custom-call(bf16[2,32,1408]{2,1,0:T(8,128)(2,1)S(1)} %multiply_convert_fusion.refs_0_), custom_call_target="tpu_custom_call" | custom-call | tf_op jit(solution)/shard_map/gather_rows/pallas_call | solution.py:239
  127.2 1.5 %collective-permute-start.3 = (bf16[88,704]{1,0:T(8,128)(2,1)S(1)}, bf16[88,704]{1,0:T(8,128)(2,1)S(1)}, u32[]{:S(2)}, u32[]{:S(2)}) collective-permute-start(bf16[88,704]{1,0:T(8,128)(2,1)S(1)} %broadcast_select_fusion.5), channel_id=1, source_target_pairs={{0,1},{1,0},{2,3},{3,2},{4,5},{5,4},{6,7},{7,6},{8,9},{9,8},{10,11... | collective-permute-start | bytes 371720 | tf_op jit(solution)/shard_map/ppermute | solution.py:395
  128.7 3.0 %multiply_add_fusion = f32[704,1408]{1,0:T(8,128)} fusion(bf16[704,1408]{1,0:T(8,128)(2,1)S(1)} %copy-done.1, bf16[704,704]{1,0:T(8,128)(2,1)S(1)} %copy-done.7, bf16[704,704]{1,0:T(8,128)(2,1)S(1)} %copy-done.5), kind=kLoop, calls=%fused_computation.1 | loop fusion | flops 7929856 | bytes 7929856 | tf_op jit(solution)/shard_map/add | solution.py:403
  131.7 1.3 collective-permute-done.3
  133.2 16.2 %all_gather.3 = bf16[704,704]{1,0:T(8,128)(2,1)S(1)} all-gather(bf16[88,704]{1,0:T(8,128)(2,1)S(1)} %add_convert_fusion), channel_id=1, replica_groups=mesh['seq'=8,'grp'=2,'dp'=2] {'seq'}, dimensions={0}, use_global_device_ids=true | all-gather | bytes 1115136 | tf_op jit(solution)/shard_map/all_gather | solution.py:399
  149.4 1.5 convert_element_type.153
  (118 shorter events, 18.7 us)
Async XLA Ops:
  0.6 9.9 %copy-start.8 = (bf16[1,128,1408]{2,1,0:T(8,128)(2,1)S(1)}, bf16[1,128,1408]{2,1,0:T(8,128)(2,1)}, u32[]{:S(2)}) copy-start(bf16[1,128,1408]{2,1,0:T(8,128)(2,1)} %param.8) | copy-start | bytes 1081348
  0.6 10.5 %copy-start.19 = (s32[1,192]{1,0:T(1,128)S(1)}, s32[1,192]{1,0:T(1,128)}, u32[]{:S(2)}) copy-start(s32[1,192]{1,0:T(1,128)} %param.10) | copy-start | bytes 2308
  0.7 10.5 %copy-start.21 = (s32[1,128]{1,0:T(1,128)S(1)}, s32[1,128]{1,0:T(1,128)}, u32[]{:S(2)}) copy-start(s32[1,128]{1,0:T(1,128)} %param.9) | copy-start | bytes 1540
  2.7 9.4 %copy-start.17 = (f32[1408]{0:T(1024)S(1)}, f32[1408]{0:T(1024)}, u32[]{:S(2)}) copy-start(f32[1408]{0:T(1024)} %param.15) | copy-start | bytes 16900
  7.5 42.7 %collective-permute-start = (bf16[704,528]{0,1:T(8,128)(2,1)}, bf16[704,528]{0,1:T(8,128)(2,1)}, u32[]{:S(2)}, u32[]{:S(2)}) collective-permute-start(bf16[704,528]{0,1:T(8,128)(2,1)} %bitcast_dynamic-update-slice_fusion), channel_id=1, source_target_pairs={{0,1},{1,0},{2,3},{3,2},{4,5},{5,4},{6,7},{7,6},{8,9},{9,8},{10,11... | collective-permute-start | bytes 2230280 | tf_op jit(solution)/shard_map/ppermute | solution.py:272
  10.5 61.6 %collective-permute-start.1 = (bf16[704,704]{1,0:T(8,128)(2,1)}, bf16[704,704]{1,0:T(8,128)(2,1)}, u32[]{:S(2)}, u32[]{:S(2)}) collective-permute-start(bf16[704,704]{1,0:T(8,128)(2,1)} %param.14), channel_id=1, source_target_pairs={{0,1},{1,0},{2,3},{3,2},{4,5},{5,4},{6,7},{7,6},{8,9},{9,8},{10,11... | collective-permute-start | bytes 2973704 | tf_op jit(solution)/shard_map/ppermute | solution.py:272
  51.8 2.2 %copy-start.2 = (bf16[704,528]{0,1:T(8,128)(2,1)}, bf16[704,528]{0,1:T(8,128)(2,1)S(1)}, u32[]{:S(2)}) copy-start(bf16[704,528]{0,1:T(8,128)(2,1)S(1)} %get-tuple-element.22) | copy-start | bytes 2230276
  51.8 2.2 %copy-start.3 = (bf16[704,528]{0,1:T(8,128)(2,1)}, bf16[704,528]{0,1:T(8,128)(2,1)S(1)}, u32[]{:S(2)}) copy-start(bf16[704,528]{0,1:T(8,128)(2,1)S(1)} %get-tuple-element.23) | copy-start | bytes 2230276
  54.1 2.7 %copy-start.14 = (bf16[1024,264]{0,1:T(8,128)(2,1)}, bf16[1024,264]{0,1:T(8,128)(2,1)S(1)}, u32[]{:S(2)}) copy-start(bf16[1024,264]{0,1:T(8,128)(2,1)S(1)} %convolution_convert_fusion.4) | copy-start | bytes 1622020
  54.1 2.7 %copy-start.15 = (bf16[256,176]{0,1:T(8,128)(2,1)S(1)}, bf16[256,176]{0,1:T(8,128)(2,1)}, u32[]{:S(2)}) copy-start(bf16[256,176]{0,1:T(8,128)(2,1)} %convolution_convert_fusion.6) | copy-start | bytes 270340
  60.1 3.4 %copy-start = (f32[1024,1024]{0,1:T(8,128)S(1)}, f32[1024,1024]{0,1:T(8,128)}, u32[]{:S(2)}) copy-start(f32[1024,1024]{0,1:T(8,128)} %get-tuple-element.44) | copy-start | bytes 12582916
  63.5 7.0 %copy-start.22 = (s32[64]{0:T(128)S(1)}, s32[64]{0:T(128)}, u32[]{:S(2)}) copy-start(s32[64]{0:T(128)} %iota_add_fusion) | copy-start | bytes 772
  66.1 17.2 %copy-start.1 = (bf16[704,1408]{1,0:T(8,128)(2,1)S(1)}, bf16[704,1408]{1,0:T(8,128)(2,1)}, u32[]{:S(2)}) copy-start(bf16[704,1408]{1,0:T(8,128)(2,1)} %param.12) | copy-start | bytes 5947396
  66.1 16.0 %all-to-all-start = ((bf16[8,128,176]{1,2,0:T(8,128)(2,1)}), bf16[8,128,176]{1,2,0:T(8,128)(2,1)}, u32[]{:S(2)}, u32[]{:S(2)}) async-start(bf16[8,128,176]{1,2,0:T(8,128)(2,1)} %copy_bitcast_fusion), calls=%async_computation | async-start | bytes 720896 | tf_op jit(solution)/shard_map/all_to_all | solution.py:348
  74.8 9.7 %copy-start.4 = (bf16[704,704]{1,0:T(8,128)(2,1)}, bf16[704,704]{1,0:T(8,128)(2,1)S(1)}, u32[]{:S(2)}) copy-start(bf16[704,704]{1,0:T(8,128)(2,1)S(1)} %get-tuple-element.20) | copy-start | bytes 2973700
  84.5 10.9 %copy-start.9 = (bf16[1,128,1408]{2,1,0:T(8,128)(2,1)S(1)}, bf16[1,128,1408]{2,1,0:T(8,128)(2,1)}, u32[]{:S(2)}) copy-start(bf16[1,128,1408]{2,1,0:T(8,128)(2,1)} %param.8) | copy-start | bytes 1081348
  84.5 10.9 %copy-start.18 = (f32[1408]{0:T(1024)S(1)}, f32[1408]{0:T(1024)}, u32[]{:S(2)}) copy-start(f32[1408]{0:T(1024)} %param.15) | copy-start | bytes 16900
  84.7 9.7 %collective-permute-start.2 = (bf16[2,64,1408]{2,1,0:T(8,128)(2,1)S(1)}, bf16[2,64,1408]{2,1,0:T(8,128)(2,1)S(1)}, u32[]{:S(2)}, u32[]{:S(2)}) collective-permute-start(bf16[2,64,1408]{2,1,0:T(8,128)(2,1)S(1)} %broadcast_select_fusion.4), channel_id=1, source_target_pairs={{0,2},{2,0},{1,3},{3,1},{4,6},{6,4},{5,7},{7,5},{8,10},{10,8},{9,1... | collective-permute-start | bytes 1081352 | tf_op jit(solution)/shard_map/ppermute | solution.py:363
  85.3 12.7 %copy-start.10 = (bf16[1,128,1408]{2,1,0:T(8,128)(2,1)S(1)}, bf16[1,128,1408]{2,1,0:T(8,128)(2,1)}, u32[]{:S(2)}) copy-start(bf16[1,128,1408]{2,1,0:T(8,128)(2,1)} %param.8) | copy-start | bytes 1081348
  94.5 5.1 %copy-start.20 = (f32[2,32]{1,0:T(2,128)S(1)}, f32[2,32]{1,0:T(2,128)}, u32[]{:S(2)}) copy-start(f32[2,32]{1,0:T(2,128)} %mul.278) | copy-start | bytes 772
  99.3 27.2 %copy-start.13 = (bf16[1024,88]{0,1:T(8,128)(2,1)S(1)}, bf16[1024,88]{0,1:T(8,128)(2,1)}, u32[]{:S(2)}) copy-start(bf16[1024,88]{0,1:T(8,128)(2,1)} %copy-done.12) | copy-start | bytes 540676
  101.1 27.6 %copy-start.5 = (bf16[704,704]{1,0:T(8,128)(2,1)S(1)}, bf16[704,704]{1,0:T(8,128)(2,1)}, u32[]{:S(2)}) copy-start(bf16[704,704]{1,0:T(8,128)(2,1)} %copy-done.4) | copy-start | bytes 2973700
  101.1 27.6 %copy-start.7 = (bf16[704,704]{1,0:T(8,128)(2,1)S(1)}, bf16[704,704]{1,0:T(8,128)(2,1)}, u32[]{:S(2)}) copy-start(bf16[704,704]{1,0:T(8,128)(2,1)} %get-tuple-element.21) | copy-start | bytes 2973700
  127.2 5.9 %collective-permute-start.3 = (bf16[88,704]{1,0:T(8,128)(2,1)S(1)}, bf16[88,704]{1,0:T(8,128)(2,1)S(1)}, u32[]{:S(2)}, u32[]{:S(2)}) collective-permute-start(bf16[88,704]{1,0:T(8,128)(2,1)S(1)} %broadcast_select_fusion.5), channel_id=1, source_target_pairs={{0,1},{1,0},{2,3},{3,2},{4,5},{5,4},{6,7},{7,6},{8,9},{9,8},{10,11... | collective-permute-start | bytes 371720 | tf_op jit(solution)/shard_map/ppermute | solution.py:395
  (4 other events, 7.1 us)

commit v3 on v2

--- a/solution.py
+++ b/solution.py
@@ -252,6 +252,127 @@
     return (results[0].reshape(shards * 2 * count, width), *results[1:])
 
 
+def middle_kernel(shards, *refs):
+    (
+        q_t, k_t, v_t, q_s, k_s, v_s, out_t, out_s, tokens_ref, seeds_ref, usable_ref,
+        back_ref, mix_s, mix_t, got_t, got_s, part_t, part_s, came_t, came_s,
+        send_t, recv_t, send_s, recv_s, y_send, y_recv,
+    ) = refs
+    me, grp = lax.axis_index("seq"), lax.axis_index("grp")
+    across = 1 - grp
+
+    barrier = pltpu.get_barrier_semaphore()
+    for k in range(1, shards):
+        peer = {"seq": lax.rem(me + k, shards)}
+        pl.semaphore_signal(barrier, inc=1, device_id=peer, device_id_type=MESH)
+    pl.semaphore_signal(barrier, inc=1, device_id={"grp": across}, device_id_type=MESH)
+    pl.semaphore_wait(barrier, shards)
+
+    def turn(k):
+        return lax.rem(me + 1 + k, shards)
+
+    def copy(k, mix, got, send, recv):
+        return pltpu.make_async_remote_copy(
+            src_ref=mix.at[turn(k)],
+            dst_ref=got.at[me],
+            send_sem=send.at[k],
+            recv_sem=recv.at[k],
+            device_id={"seq": turn(k)},
+            device_id_type=MESH,
+        )
+
+    def heads(queries, keys, values, mix, got, send, recv):
+        def step(k, carry):
+            dest = turn(k)
+            mix[dest] = attend(queries[dest], keys[...], values[...])
+
+            @pl.when(k > 0)
+            def _():
+                copy(k - 1, mix, got, send, recv).start()
+
+            return carry
+
+        lax.fori_loop(0, shards, step, 0)
+        got[me] = mix[me]
+
+    def y_copy(index, part, came):
+        return pltpu.make_async_remote_copy(
+            src_ref=part.at[across],
+            dst_ref=came,
+            send_sem=y_send.at[index],
+            recv_sem=y_recv.at[index],
+            device_id={"grp": across},
+            device_id_type=MESH,
+        )
+
+    def project(got, weights, part):
+        rows = jnp.concatenate([got[k] for k in range(shards)], axis=1)
+        whole = dot32(rows, weights[...]).astype(jnp.bfloat16)
+        half = whole.shape[0] // 2
+        part[0] = whole[:half]
+        part[1] = whole[half:]
+
+    def total(part, came):
+        return part[grp].astype(jnp.float32) + came[...].astype(jnp.float32)
+
+    heads(q_t, k_t, v_t, mix_t, got_t, send_t, recv_t)
+    heads(q_s, k_s, v_s, mix_s, got_s, send_s, recv_s)
+    for k in range(shards - 1):
+        copy(k, mix_t, got_t, send_t, recv_t).wait_recv()
+    project(got_t, out_t, part_t)
+    copy(0, mix_s, got_s, send_s, recv_s).wait_recv()
+    y_copy(0, part_t, came_t).start()
+    for k in range(1, shards - 1):
+        copy(k, mix_s, got_s, send_s, recv_s).wait_recv()
+    project(got_s, out_s, part_s)
+    y_copy(0, part_t, came_t).wait_recv()
+    y_copy(1, part_s, came_s).start()
+    tokens = tokens_ref[...].astype(jnp.float32)
+    features = layer_norm(tokens + total(part_t, came_t))[0].astype(jnp.bfloat16)
+    y_copy(1, part_s, came_s).wait_recv()
+    predicted, factor = layer_norm(seeds_ref[...] + total(part_s, came_s))
+    back_ref[...] = gradient(predicted, factor, features, usable_ref[...]).astype(jnp.bfloat16)
+    for k in range(shards - 1):
+        copy(k, mix_t, got_t, send_t, recv_t).wait_send()
+        copy(k, mix_s, got_s, send_s, recv_s).wait_send()
+    y_copy(0, part_t, came_t).wait_send()
+    y_copy(1, part_s, came_s).wait_send()
+
+
+def middle(shards, operands):
+    q_t = operands[0]
+    rows, width = operands[8].shape
+    bf16, dma = jnp.bfloat16, pltpu.SemaphoreType.DMA
+    vmem = pl.BlockSpec(memory_space=pltpu.VMEM)
+    return pl.pallas_call(
+        functools.partial(middle_kernel, shards),
+        out_shape=[
+            jax.ShapeDtypeStruct((rows, width), bf16),
+            jax.ShapeDtypeStruct(q_t.shape, bf16),
+        ],
+        in_specs=[vmem] * len(operands),
+        out_specs=[vmem] * 2,
+        scratch_shapes=[pltpu.VMEM(q_t.shape, bf16)] * 3
+        + [pltpu.VMEM((2, rows, width), bf16)] * 2
+        + [pltpu.VMEM((rows, width), bf16)] * 2
+        + [dma((shards - 1,))] * 4
+        + [dma((2,))] * 2,
+        name="middle",
+        compiler_params=pltpu.CompilerParams(
+            collective_id=3, has_side_effects=True, vmem_limit_bytes=48 * 1024 * 1024
+        ),
+    )(*operands)
+
+
+def gradient(predicted, factor, features, usable):
+    slope = jnp.clip(predicted - features.astype(jnp.float32), -1.0, 1.0) * usable
+    return (
+        slope
+        - jnp.mean(slope, axis=1, keepdims=True)
+        - predicted * jnp.mean(slope * predicted, axis=1, keepdims=True)
+    ) * factor
+
+
 def attend(queries, keys, values):
     scores = lax.dot_general(
         queries, keys, (((1,), (1,)), ((), ())), preferred_element_type=jnp.float32
@@ -293,8 +414,7 @@
         return lax.dynamic_slice_in_dim(weights, head * HEAD_DIM, HEAD_DIM, axis=2)
 
     mine = jnp.concatenate([columns(target_qkv), columns(student_qkv)], axis=0)
-    mine = jnp.concatenate([mine[k] for k in range(6)], axis=1)
-    weights = both_of_dp(mine, 0)
+    weights = both_of_dp(mine, 1)
     relaid = both_of_dp(student_out, 1)
 
     grp = lax.axis_index("grp")
@@ -315,16 +435,17 @@
             return rows
         return lax.dynamic_slice_in_dim(rows, part * part_rows, part_rows, axis=0)
 
-    pick = lambda k: weights[:, k * HEAD_DIM : (k + 1) * HEAD_DIM]
-    seed_queries = dot32(own_part(seed_normed), pick(3)).astype(jnp.bfloat16)
+    def project(rows, some):
+        return jnp.einsum(
+            "nr,krc->knc", rows, some, preferred_element_type=jnp.float32
+        ).astype(jnp.bfloat16)
+
+    seed_queries = dot32(own_part(seed_normed), weights[3]).astype(jnp.bfloat16)
     if rep == 1:
-        triple = dot32(every, weights[:, : 3 * HEAD_DIM]).astype(jnp.bfloat16)
-        query_t = triple[:, :HEAD_DIM]
-        pair_t = triple[:, HEAD_DIM:]
+        query_t, key_t, value_t = project(every, weights[:3])
     else:
-        query_t = dot32(own_part(every), pick(0)).astype(jnp.bfloat16)
-        pair_t = dot32(every, weights[:, HEAD_DIM : 3 * HEAD_DIM]).astype(jnp.bfloat16)
-    target_mixed = attend(query_t, pair_t[:, :HEAD_DIM], pair_t[:, HEAD_DIM:])
+        query_t = dot32(own_part(every), weights[0]).astype(jnp.bfloat16)
+        key_t, value_t = project(every, weights[1:3])
 
     is_context = flags == 1
     order = jnp.cumsum(is_context.astype(jnp.int32), axis=1) - 1
@@ -339,31 +460,8 @@
         preferred_element_type=jnp.float32,
     ).astype(jnp.bfloat16)
     chosen = chosen.reshape(shards * CTX_DEV, width)
-    pair_s = dot32(chosen, weights[:, 4 * HEAD_DIM :]).astype(jnp.bfloat16)
-    student_mixed = attend(seed_queries, pair_s[:, :HEAD_DIM], pair_s[:, HEAD_DIM:])
-
-    both = jnp.concatenate([target_mixed, student_mixed], axis=1)
-    if rep == 1:
-        both = both.reshape(shards, row_count, 2 * HEAD_DIM)
-        both = lax.all_to_all(both, "seq", split_axis=0, concat_axis=0, tiled=True)
-    else:
-        both = lax.all_gather(both, "seq", axis=0, tiled=True)
-        both = both.reshape(head_count, length, 2 * HEAD_DIM)
-        both = lax.dynamic_slice_in_dim(both, me * row_count, row_count, axis=1)
-    own_target = both[:, :, :HEAD_DIM].transpose(1, 0, 2).reshape(row_count, half_width)
-    own_student = both[:, :, HEAD_DIM:].transpose(1, 0, 2).reshape(row_count, half_width)
-    sums = jnp.stack(
-        [
-            dot32(own_target, target_out).astype(jnp.bfloat16),
-            dot32(own_student, relaid).astype(jnp.bfloat16),
-        ]
-    )
-    low, high = sums[:, :half_rows], sums[:, half_rows:]
-    keep, send = jnp.where(grp == 0, low, high), jnp.where(grp == 0, high, low)
-    came = lax.ppermute(send, "grp", [(0, 1), (1, 0)])
-    sums = keep.astype(jnp.float32) + came.astype(jnp.float32)
-
-    features = layer_norm(own_tokens + sums[0])[0].astype(jnp.bfloat16)
+    key_s, value_s = project(chosen, weights[4:])
+
     base = me * row_count + grp * half_rows
     first, second, twice_c, twice_s = tables
     blocks = half_rows // STRIDE
@@ -371,15 +469,48 @@
     second = lax.dynamic_slice_in_dim(second, base // STRIDE, blocks, axis=0)
     own_seeds = first[:, None] * twice_c[None] + second[:, None] * twice_s[None]
     own_seeds = mask_token[None, :] + own_seeds.reshape(half_rows, width)
-    predicted, factor = layer_norm(own_seeds + sums[1])
     places = base + jnp.arange(half_rows, dtype=jnp.int32)
-    usable = jnp.sum((lists[None, :] == places[:, None]).astype(jnp.float32), axis=1)
-    slope = jnp.clip(predicted - features.astype(jnp.float32), -1.0, 1.0) * usable[:, None]
-    back_grad = (
-        slope
-        - jnp.mean(slope, axis=1, keepdims=True)
-        - predicted * jnp.mean(slope * predicted, axis=1, keepdims=True)
-    ) * factor
+    usable = jnp.sum(
+        (lists[None, :] == places[:, None]).astype(jnp.float32), axis=1, keepdims=True
+    )
+    if rep == 1:
+        blocked = (shards, row_count, HEAD_DIM)
+        back_grad, student_mixed = middle(
+            shards,
+            [
+                query_t.reshape(blocked), key_t, value_t,
+                seed_queries.reshape(blocked), key_s, value_s,
+                target_out, relaid, own_tokens, own_seeds, usable,
+            ],
+        )
+        student_mixed = student_mixed.reshape(length, HEAD_DIM)
+    else:
+        target_mixed = attend(query_t, key_t, value_t)
+        student_mixed = attend(seed_queries, key_s, value_s)
+        both = jnp.concatenate([target_mixed, student_mixed], axis=1)
+        if rep == 1:
+            both = both.reshape(shards, row_count, 2 * HEAD_DIM)
+            both = lax.all_to_all(both, "seq", split_axis=0, concat_axis=0, tiled=True)
+        else:
+            both = lax.all_gather(both, "seq", axis=0, tiled=True)
+            both = both.reshape(head_count, length, 2 * HEAD_DIM)
+            both = lax.dynamic_slice_in_dim(both, me * row_count, row_count, axis=1)
+        own_target = both[:, :, :HEAD_DIM].transpose(1, 0, 2).reshape(row_count, half_width)
+        own_student = both[:, :, HEAD_DIM:].transpose(1, 0, 2).reshape(row_count, half_width)
+        sums = jnp.stack(
+            [
+                dot32(own_target, target_out).astype(jnp.bfloat16),
+                dot32(own_student, relaid).astype(jnp.bfloat16),
+            ]
+        )
+        low, high = sums[:, :half_rows], sums[:, half_rows:]
+        keep, send = jnp.where(grp == 0, low, high), jnp.where(grp == 0, high, low)
+        came = lax.ppermute(send, "grp", [(0, 1), (1, 0)])
+        sums = keep.astype(jnp.float32) + came.astype(jnp.float32)
+
+        features = layer_norm(own_tokens + sums[0])[0].astype(jnp.bfloat16)
+        predicted, factor = layer_norm(own_seeds + sums[1])
+        back_grad = gradient(predicted, factor, features, usable)
     back_all = gather_rows(back_grad.astype(jnp.bfloat16), shards)[0]
     head_grad = lax.dot_general(
         student_mixed,

time: 151 us -> 143 us (0.947)
  Pallas kernels: 59.4 us -> 88.3 us
  waiting for transfers between devices: 17.8 us -> 4.37 us
  other arithmetic: 22.1 us -> 13.4 us
  matrix products: 13 us -> 7.33 us
  starting transfers between devices: 9.5 us -> 4.53 us
  local copies, waits for them, and re-layouts: 11.8 us -> 8.12 us
    pallas_call x0 -> x1, Pallas kernels: none -> 24.9 us  [middle(): pl.pallas_call(functools.partial(middle_kernel, shards), out_shape=[jax.S...]
    ppermute x1 -> x0, waiting for transfers between devices: 9.1 us -> none  [body(): came = lax.ppermute(send, 'grp', [(0, 1), (1, 0)])]
    all_to_all x1 -> x0, waiting for transfers between devices: 7.37 us -> none  [body(): both = lax.all_to_all(both, 'seq', split_axis=0, concat_axis=0, tiled=True)]
    dot_general x4 -> x2, matrix products: 7.92 us -> 2.27 us  [project(): jnp.einsum('nr,krc->knc', rows, some, preferred_element_type=jnp.float32)]
    reduce_sum x4 -> x1, other arithmetic: 4.75 us -> 0.21 us  [body(): jnp.sum((lists[None, :] == places[:, None]).astype(jnp.float32), axis=1,...]
    all_to_all x1 -> x0, starting transfers between devices: 4.4 us -> none  [body(): both = lax.all_to_all(both, 'seq', split_axis=0, concat_axis=0, tiled=True)]
    slice x3 -> x0, local copies, waits for them, and re-layouts: 4.04 us -> none  [the longest x1 2 us: body(): mine = jnp.concatenate([mine[k] for k in range(6)], axis=1)]
    pallas_call x2, Pallas kernels: 59.4 us -> 63.3 us  [gather_rows(): pl.pallas_call(functools.partial(gather_kernel, shards, with_seeds), out_...]
  transfers between devices with their start and end apart: 5 -> 3, of which waited for: 3 -> 1; matrix products, arithmetic and copies ran while one was open for 19% -> 11% of each run, Pallas kernels for 23% -> 24%
where the time goes in v3:
time: 143 us
  Pallas kernels  88.3 us (62%)
  blocking collectives  15.8 us (11%)
  other arithmetic  13.4 us (9%)
  local copies, waits for them, and re-layouts  8.12 us (6%)
  matrix products  7.33 us (5%)
  starting transfers between devices  4.53 us (3%)
  waiting for transfers between devices  4.37 us (3%)
    pallas_call x2, Pallas kernels, gather_rows(): pl.pallas_call(functools.partial(gather_kernel, shards, with_seeds), out_...  63.3 us
    pallas_call x1, Pallas kernels, middle(): pl.pallas_call(functools.partial(middle_kernel, shards), out_shape=[jax.S...  24.9 us
    all_gather x1, blocking collectives, body(): lax.all_gather(head_grad, 'seq', axis=0, tiled=True).astype(jnp.float32)  15.8 us
    ppermute x1, waiting for transfers between devices, body(): came = lax.ppermute(send, 'dp', [(0, 1), (1, 0)])  4.37 us
    add x1, other arithmetic, body(): MOMENTUM * target_out.astype(jnp.float32)  3.85 us
    select_n x2, other arithmetic, both_of_dp(): jnp.where(first, block, other)  3.05 us
    dot_general x1, matrix products, dot32(): return jnp.dot(left, right, preferred_element_type=jnp.float32)  3.04 us
    ppermute x2, starting transfers between devices, both_of_dp(): other = lax.ppermute(block, 'dp', [(0, 1), (1, 0)])  2.99 us
  transfers between devices with their start and end apart: 3, of which 1 were waited for; matrix products, arithmetic and copies ran while one was open for 11% of the time, Pallas kernels for 24%

profile of v3, /device:TPU:0, one launch (start us, length us, event | category | flops | bytes accessed | tf_op | source)
XLA Modules:
  0.0 142.8 jit_solution(5959135209409576520)
XLA Ops:
  0.6 2.0 %constant_dynamic-slice_fusion = (bf16[3,704,88]{2,1,0:T(8,128)(2,1)S(1)}, bf16[3,704,88]{2,1,0:T(8,128)(2,1)S(1)}) fusion(bf16[3,704,704]{2,1,0:T(8,128)(2,1)} %param.13, s32[]{:T(128)S(6)} %select_n.56, bf16[3,704,704]{2,1,0:T(8,128)(2,1)} %param.11), kind=kLoop, calls=%fused_computation.54 | loop fusion | bytes 1486852 | tf_op jit(solution)/shard_map/dynamic_slice | solution.py:414
  3.2 1.0 pad_maximum_fusion.4
  4.2 3.0 %collective-permute-start = (bf16[6,704,88]{1,2,0:T(8,128)(2,1)}, bf16[6,704,88]{1,2,0:T(8,128)(2,1)}, u32[]{:S(2)}, u32[]{:S(2)}) collective-permute-start(bf16[6,704,88]{1,2,0:T(8,128)(2,1)} %pad_maximum_fusion.4), channel_id=1, source_target_pairs={{0,1},{1,0},{2,3},{3,2},{4,5},{5,4},{6,7},{7,6},{8,9},{9,8},{10,11... | collective-permute-start | bytes 2230280 | tf_op jit(solution)/shard_map/ppermute | solution.py:393
  7.2 0.8 convert_bitcast_fusion
  8.6 0.8 multiply_sine_fusion
  10.0 33.9 %gather_seeds.1 = (bf16[8,2,2,32,1408]{4,3,2,1,0:T(8,128)(2,1)S(1)}, s32[8,8,384]{2,1,0:T(8,128)S(1)}, bf16[1024,1408]{1,0:T(8,128)(2,1)}) custom-call(bf16[2,32,1408]{2,1,0:T(8,128)(2,1)S(1)} %multiply_convert_fusion.refs_0_, s32[8,384]{1,0:T(8,128)S(1)} %pad.4.refs_1_, f32[32,1408]{1,0:T(8,128)S(1)} %get-tuple-element.30.refs_2_, ...), custom_call_target="tpu_custom_call" | custom-call | tf_op jit(solution)/shard_map/gather_seeds/pallas_call | solution.py:239
  44.3 0.9 fusion.8
  45.6 1.4 convolution_convert_fusion
  47.1 1.3 broadcast_select_fusion.3
  48.5 0.9 copy-done.2
  49.6 1.9 %convolution_convert_fusion.2 = bf16[3,88,1024]{2,1,0:T(8,128)(2,1)} fusion(bf16[1024,1408,1]{1,0,2:T(8,128)(2,1)S(1)} %bitcast.46, bf16[6,704,88]{1,2,0:T(8,128)(2,1)S(1)} %get-tuple-element.19, bf16[6,704,88]{1,2,0:T(8,128)(2,1)S(1)} %get-tuple-element.18), kind=kOutput, calls=%fused_computation.5 | convolution fusion | flops 764510208 | bytes 4911104 | tf_op jit(solution)/shard_map/nr,krc->knc/dot_general | solution.py:439
  51.5 2.2 %copy.24 = bf16[3,88,1024]{1,2,0:T(8,128)(2,1)} copy(bf16[3,88,1024]{2,1,0:T(8,128)(2,1)} %convolution_convert_fusion.2) | data formatting | bytes 1081344 | tf_op jit(solution)/shard_map/convert_element_type | solution.py:441
  53.7 3.0 %convolution_convert_fusion.3 = bf16[1024,88]{0,1:T(8,128)(2,1)S(1)} fusion(bf16[1024,1408]{1,0:T(8,128)(2,1)} %get-tuple-element.8, bf16[6,704,88]{1,2,0:T(8,128)(2,1)} %copy-done.4, bf16[6,704,88]{1,2,0:T(8,128)(2,1)} %copy-done.2), kind=kOutput, calls=%fused_computation.6 | convolution fusion | flops 254341120 | bytes 4550656 | tf_op jit(solution)/shard_map/dot_general | solution.py:387
  57.0 0.4 convolution_convert_fusion.4
  57.5 1.3 slice_bitcast_fusion
  58.8 1.7 %broadcast_select_fusion.1 = (bf16[704,704]{1,0:T(8,128)(2,1)S(1)}, bf16[704,704]{1,0:T(8,128)(2,1)S(1)}) fusion(bf16[704,704]{1,0:T(8,128)(2,1)} %param.14, bf16[704,704]{1,0:T(8,128)(2,1)} %collective-permute-done.1, pred[]{:T(512)S(6)} %eq.36), kind=kLoop, calls=%fused_computation.9 | loop fusion | flops 991232 | bytes 3964929 | tf_op jit(solution)/shard_map/jit(_where)/select_n | solution.py:396
  60.6 3.8 %multiply_add_fusion = (f32[704,1408]{1,0:T(8,128)}, bf16[704,1408]{1,0:T(8,128)(2,1)}) fusion(bf16[704,1408]{1,0:T(8,128)(2,1)S(1)} %copy-done, bf16[704,704]{1,0:T(8,128)(2,1)S(1)} %get-tuple-element.17, bf16[704,704]{1,0:T(8,128)(2,1)S(1)} %get-tuple-element.16), kind=kLoop, calls=%fused_computation | loop fusion | flops 8921088 | bytes 9912320 | tf_op jit(solution)/shard_map/add | solution.py:534
  64.4 24.9 %middle.1 = (bf16[64,1408]{1,0:T(8,128)(2,1)S(1)}, bf16[8,128,88]{2,1,0:T(8,128)(2,1)S(1)}) custom-call(bf16[8,128,88]{2,1,0:T(8,128)(2,1)S(1)} %bitcast.48, bf16[1024,88]{1,0:T(8,128)(2,1)S(1)} %get-tuple-element.21.refs_1_, bf16[1024,88]{1,0:T(8,128)(2,1)S(1)} %get-tuple-element.20.refs_2_, bf16[8,128,88]{2,1,0:T(8,128)(2,1)S(1)} %bitcast.47, ...), custom_call_target="tpu_custom_call" | custom-call | tf_op jit(solution)/shard_map/middle/pallas_call | solution.py:347
  89.4 29.4 %gather_rows.1 = bf16[8,2,2,32,1408]{4,3,2,1,0:T(8,128)(2,1)S(1)} custom-call(bf16[2,32,1408]{2,1,0:T(8,128)(2,1)S(1)} %bitcast.50), custom_call_target="tpu_custom_call" | custom-call | tf_op jit(solution)/shard_map/gather_rows/pallas_call | solution.py:239
  118.8 0.6 convolution_convert_fusion.1
  119.5 1.5 %collective-permute-start.2 = (bf16[88,704]{1,0:T(8,128)(2,1)S(1)}, bf16[88,704]{1,0:T(8,128)(2,1)S(1)}, u32[]{:S(2)}, u32[]{:S(2)}) collective-permute-start(bf16[88,704]{1,0:T(8,128)(2,1)S(1)} %broadcast_select_fusion.4), channel_id=1, source_target_pairs={{0,1},{1,0},{2,3},{3,2},{4,5},{5,4},{6,7},{7,6},{8,9},{9,8},{10,11... | collective-permute-start | bytes 371720 | tf_op jit(solution)/shard_map/ppermute | solution.py:526
  121.0 4.4 %collective-permute-done.2 = bf16[88,704]{1,0:T(8,128)(2,1)S(1)} collective-permute-done((bf16[88,704]{1,0:T(8,128)(2,1)S(1)}, bf16[88,704]{1,0:T(8,128)(2,1)S(1)}, u32[]{:S(2)}, u32[]{:S(2)}) %collective-permute-start.2) | collective-permute-done | bytes 123936 | tf_op jit(solution)/shard_map/ppermute | solution.py:526
  125.5 15.8 %all_gather.3 = bf16[704,704]{1,0:T(8,128)(2,1)S(1)} all-gather(bf16[88,704]{1,0:T(8,128)(2,1)S(1)} %add_convert_fusion), channel_id=1, replica_groups=mesh['seq'=8,'grp'=2,'dp'=2] {'seq'}, dimensions={0}, use_global_device_ids=true | all-gather | bytes 1115136 | tf_op jit(solution)/shard_map/all_gather | solution.py:530
  141.3 1.5 %convert_element_type.104 = f32[704,704]{1,0:T(8,128)} convert(bf16[704,704]{1,0:T(8,128)(2,1)S(1)} %all_gather.3) | non-fusion elementwise | flops 495616 | bytes 2973696 | tf_op jit(solution)/shard_map/convert_element_type | solution.py:530
  (69 shorter events, 3.3 us)
Async XLA Ops:
  0.6 6.6 %copy-start.12 = (bf16[1,128,1408]{2,1,0:T(8,128)(2,1)S(1)}, bf16[1,128,1408]{2,1,0:T(8,128)(2,1)}, u32[]{:S(2)}) copy-start(bf16[1,128,1408]{2,1,0:T(8,128)(2,1)} %param.8) | copy-start | bytes 1081348
  2.7 5.9 %copy-start.14 = (s32[1,192]{1,0:T(1,128)S(1)}, s32[1,192]{1,0:T(1,128)}, u32[]{:S(2)}) copy-start(s32[1,192]{1,0:T(1,128)} %param.10) | copy-start | bytes 2308
  2.7 5.9 %copy-start.15 = (s32[1,128]{1,0:T(1,128)S(1)}, s32[1,128]{1,0:T(1,128)}, u32[]{:S(2)}) copy-start(s32[1,128]{1,0:T(1,128)} %param.9) | copy-start | bytes 1540
  2.7 6.8 %copy-start.13 = (f32[1408]{0:T(1024)S(1)}, f32[1408]{0:T(1024)}, u32[]{:S(2)}) copy-start(f32[1408]{0:T(1024)} %param.15) | copy-start | bytes 16900
  3.0 6.4 %copy-start.6 = (bf16[3,704,88]{1,2,0:T(8,128)(2,1)}, bf16[3,704,88]{1,2,0:T(8,128)(2,1)S(1)}, u32[]{:S(2)}) copy-start(bf16[3,704,88]{1,2,0:T(8,128)(2,1)S(1)} %copy.30) | copy-start | bytes 1115140
  3.2 6.6 %copy-start.8 = (bf16[3,704,88]{1,2,0:T(8,128)(2,1)}, bf16[3,704,88]{1,2,0:T(8,128)(2,1)S(1)}, u32[]{:S(2)}) copy-start(bf16[3,704,88]{1,2,0:T(8,128)(2,1)S(1)} %copy.29) | copy-start | bytes 1115140
  4.2 42.9 %collective-permute-start = (bf16[6,704,88]{1,2,0:T(8,128)(2,1)}, bf16[6,704,88]{1,2,0:T(8,128)(2,1)}, u32[]{:S(2)}, u32[]{:S(2)}) collective-permute-start(bf16[6,704,88]{1,2,0:T(8,128)(2,1)} %pad_maximum_fusion.4), channel_id=1, source_target_pairs={{0,1},{1,0},{2,3},{3,2},{4,5},{5,4},{6,7},{7,6},{8,9},{9,8},{10,11... | collective-permute-start | bytes 2230280 | tf_op jit(solution)/shard_map/ppermute | solution.py:393
  7.2 51.6 %collective-permute-start.1 = (bf16[704,704]{1,0:T(8,128)(2,1)}, bf16[704,704]{1,0:T(8,128)(2,1)}, u32[]{:S(2)}, u32[]{:S(2)}) collective-permute-start(bf16[704,704]{1,0:T(8,128)(2,1)} %param.14), channel_id=1, source_target_pairs={{0,1},{1,0},{2,3},{3,2},{4,5},{5,4},{6,7},{7,6},{8,9},{9,8},{10,11... | collective-permute-start | bytes 2973704 | tf_op jit(solution)/shard_map/ppermute | solution.py:393
  9.4 0.6 copy-start.11
  45.6 1.5 %copy-start.7 = (bf16[3,704,88]{1,2,0:T(8,128)(2,1)S(1)}, bf16[3,704,88]{1,2,0:T(8,128)(2,1)}, u32[]{:S(2)}) copy-start(bf16[3,704,88]{1,2,0:T(8,128)(2,1)} %copy-done.6) | copy-start | bytes 1115140
  45.6 1.5 %copy-start.9 = (bf16[3,704,88]{1,2,0:T(8,128)(2,1)S(1)}, bf16[3,704,88]{1,2,0:T(8,128)(2,1)}, u32[]{:S(2)}) copy-start(bf16[3,704,88]{1,2,0:T(8,128)(2,1)} %copy-done.8) | copy-start | bytes 1115140
  48.5 0.9 copy-start.2
  48.5 1.1 copy-start.4
  53.7 3.2 %copy-start.3 = (bf16[6,704,88]{1,2,0:T(8,128)(2,1)S(1)}, bf16[6,704,88]{1,2,0:T(8,128)(2,1)}, u32[]{:S(2)}) copy-start(bf16[6,704,88]{1,2,0:T(8,128)(2,1)} %copy-done.2) | copy-start | bytes 2230276
  53.7 3.2 %copy-start.5 = (bf16[6,704,88]{1,2,0:T(8,128)(2,1)S(1)}, bf16[6,704,88]{1,2,0:T(8,128)(2,1)}, u32[]{:S(2)}) copy-start(bf16[6,704,88]{1,2,0:T(8,128)(2,1)} %copy-done.4) | copy-start | bytes 2230276
  53.7 3.3 %copy-start.10 = (bf16[8,32,1408]{2,1,0:T(8,128)(2,1)S(1)}, bf16[8,32,1408]{2,1,0:T(8,128)(2,1)}, u32[]{:S(2)}) copy-start(bf16[8,32,1408]{2,1,0:T(8,128)(2,1)} %convolution_convert_fusion) | copy-start | bytes 2162692
  57.5 3.0 %copy-start = (bf16[704,1408]{1,0:T(8,128)(2,1)S(1)}, bf16[704,1408]{1,0:T(8,128)(2,1)}, u32[]{:S(2)}) copy-start(bf16[704,1408]{1,0:T(8,128)(2,1)} %refs_6_.1) | copy-start | bytes 5947396
  60.6 3.9 %copy-start.1 = (f32[64,1408]{1,0:T(8,128)S(1)}, f32[64,1408]{1,0:T(8,128)}, u32[]{:S(2)}) copy-start(f32[64,1408]{1,0:T(8,128)} %get-tuple-element.23.refs_8_) | copy-start | bytes 1081348
  119.5 5.9 %collective-permute-start.2 = (bf16[88,704]{1,0:T(8,128)(2,1)S(1)}, bf16[88,704]{1,0:T(8,128)(2,1)S(1)}, u32[]{:S(2)}, u32[]{:S(2)}) collective-permute-start(bf16[88,704]{1,0:T(8,128)(2,1)S(1)} %broadcast_select_fusion.4), channel_id=1, source_target_pairs={{0,1},{1,0},{2,3},{3,2},{4,5},{5,4},{6,7},{7,6},{8,9},{9,8},{10,11... | collective-permute-start | bytes 371720 | tf_op jit(solution)/shard_map/ppermute | solution.py:526

commit v4 on v3

--- a/solution.py
+++ b/solution.py
@@ -89,17 +89,22 @@
 
     def z_copy(way, dist, piece):
         sign = 1 - 2 * way
-        to = {"seq": (z + sign * dist) * 2 + core}
+        slot = (z - sign * (dist - 1)) * 2 + core
+        src = x_ref.at[piece] if dist == 1 else out_ref.at[slot, grp, piece]
         return remote(
-            x_ref.at[piece], me, grp, piece,
-            z_send.at[way, dist - 1, piece], z_recv.at[way, dist - 1, piece], to,
-        )
+            src, slot, grp, piece,
+            z_send.at[way, dist - 1, piece], z_recv.at[way, dist - 1, piece],
+            {"seq": (z + sign) * 2 + core},
+        )
+
+    def comes(way, dist):
+        return z >= dist if way == 0 else z + dist < depth
+
+    def leaves(way):
+        return z + 1 < depth if way == 0 else z >= 1
 
     def goes(way, dist):
-        return z + dist < depth if way == 0 else z - dist >= 0
-
-    def comes(way, dist):
-        return goes(1 - way, dist)
+        return leaves(way) if dist == 1 else leaves(way) & comes(way, dist - 1)
 
     def mate_copy(src, source, side, piece):
         group = grp if side == 0 else across
@@ -124,13 +129,12 @@
             device_id_type=MESH,
         )
 
-    for dist in range(1, depth):
-        for way in range(2):
-
-            @pl.when(goes(way, dist))
-            def _():
-                for piece in pieces:
-                    z_copy(way, dist, piece).start()
+    for way in range(2):
+
+        @pl.when(goes(way, 1))
+        def _():
+            for piece in pieces:
+                z_copy(way, 1, piece).start()
 
     for piece in pieces:
         y_copy(x_ref.at[piece], z, piece).start()
@@ -161,6 +165,12 @@
         def _():
             for piece in pieces:
                 z_copy(way, dist, piece).wait_recv()
+                if dist + 1 < depth:
+
+                    @pl.when(leaves(way))
+                    def _():
+                        z_copy(way, dist + 1, piece).start()
+
                 held = out_ref.at[source * 2 + core, grp, piece]
                 y_copy(held, source, piece).start()
                 mate_copy(held, source, 0, piece).start()
@@ -254,8 +264,8 @@
 
 def middle_kernel(shards, *refs):
     (
-        q_t, k_t, v_t, q_s, k_s, v_s, out_t, out_s, tokens_ref, seeds_ref, usable_ref,
-        back_ref, mix_s, mix_t, got_t, got_s, part_t, part_s, came_t, came_s,
+        every, seeded, chosen, weights, out_t, out_s, tokens_ref, seeds_ref, usable_ref,
+        back_ref, mix_s, k_t, v_t, k_s, v_s, mix_t, got_t, got_s, part_t, part_s, came_t, came_s,
         send_t, recv_t, send_s, recv_s, y_send, y_recv,
     ) = refs
     me, grp = lax.axis_index("seq"), lax.axis_index("grp")
@@ -281,10 +291,14 @@
             device_id_type=MESH,
         )
 
-    def heads(queries, keys, values, mix, got, send, recv):
+    def narrow(rows, index):
+        return dot32(rows, weights[index]).astype(jnp.bfloat16)
+
+    def heads(source, index, keys, values, mix, got, send, recv):
         def step(k, carry):
             dest = turn(k)
-            mix[dest] = attend(queries[dest], keys[...], values[...])
+            queries = narrow(source[dest], index)
+            mix[dest] = attend(queries, keys[...], values[...])
 
             @pl.when(k > 0)
             def _():
@@ -315,8 +329,17 @@
     def total(part, came):
         return part[grp].astype(jnp.float32) + came[...].astype(jnp.float32)
 
-    heads(q_t, k_t, v_t, mix_t, got_t, send_t, recv_t)
-    heads(q_s, k_s, v_s, mix_s, got_s, send_s, recv_s)
+    def pair(k, carry):
+        rows = pl.ds(pl.multiple_of(k * every.shape[1], every.shape[1]), every.shape[1])
+        k_t[rows, :] = narrow(every[k], 1)
+        v_t[rows, :] = narrow(every[k], 2)
+        return carry
+
+    lax.fori_loop(0, shards, pair, 0)
+    heads(every, 0, k_t, v_t, mix_t, got_t, send_t, recv_t)
+    k_s[...] = narrow(chosen[...], 4)
+    v_s[...] = narrow(chosen[...], 5)
+    heads(seeded, 3, k_s, v_s, mix_s, got_s, send_s, recv_s)
     for k in range(shards - 1):
         copy(k, mix_t, got_t, send_t, recv_t).wait_recv()
     project(got_t, out_t, part_t)
@@ -340,19 +363,23 @@
 
 
 def middle(shards, operands):
-    q_t = operands[0]
-    rows, width = operands[8].shape
+    blocked = operands[0].shape[:2] + (HEAD_DIM,)
+    flat = (blocked[0] * blocked[1], HEAD_DIM)
+    some = (operands[2].shape[0], HEAD_DIM)
+    rows, width = operands[6].shape
     bf16, dma = jnp.bfloat16, pltpu.SemaphoreType.DMA
     vmem = pl.BlockSpec(memory_space=pltpu.VMEM)
     return pl.pallas_call(
         functools.partial(middle_kernel, shards),
         out_shape=[
             jax.ShapeDtypeStruct((rows, width), bf16),
-            jax.ShapeDtypeStruct(q_t.shape, bf16),
+            jax.ShapeDtypeStruct(blocked, bf16),
         ],
         in_specs=[vmem] * len(operands),
         out_specs=[vmem] * 2,
-        scratch_shapes=[pltpu.VMEM(q_t.shape, bf16)] * 3
+        scratch_shapes=[pltpu.VMEM(flat, bf16)] * 2
+        + [pltpu.VMEM(some, bf16)] * 2
+        + [pltpu.VMEM(blocked, bf16)] * 3
         + [pltpu.VMEM((2, rows, width), bf16)] * 2
         + [pltpu.VMEM((rows, width), bf16)] * 2
         + [dma((shards - 1,))] * 4
@@ -439,13 +466,6 @@
         return jnp.einsum(
             "nr,krc->knc", rows, some, preferred_element_type=jnp.float32
         ).astype(jnp.bfloat16)
-
-    seed_queries = dot32(own_part(seed_normed), weights[3]).astype(jnp.bfloat16)
-    if rep == 1:
-        query_t, key_t, value_t = project(every, weights[:3])
-    else:
-        query_t = dot32(own_part(every), weights[0]).astype(jnp.bfloat16)
-        key_t, value_t = project(every, weights[1:3])
 
     is_context = flags == 1
     order = jnp.cumsum(is_context.astype(jnp.int32), axis=1) - 1
@@ -460,7 +480,6 @@
         preferred_element_type=jnp.float32,
     ).astype(jnp.bfloat16)
     chosen = chosen.reshape(shards * CTX_DEV, width)
-    key_s, value_s = project(chosen, weights[4:])
 
     base = me * row_count + grp * half_rows
     first, second, twice_c, twice_s = tables
@@ -474,17 +493,20 @@
         (lists[None, :] == places[:, None]).astype(jnp.float32), axis=1, keepdims=True
     )
     if rep == 1:
-        blocked = (shards, row_count, HEAD_DIM)
+        blocked = (shards, row_count, width)
         back_grad, student_mixed = middle(
             shards,
             [
-                query_t.reshape(blocked), key_t, value_t,
-                seed_queries.reshape(blocked), key_s, value_s,
+                every.reshape(blocked), seed_normed.reshape(blocked), chosen, weights,
                 target_out, relaid, own_tokens, own_seeds, usable,
             ],
         )
         student_mixed = student_mixed.reshape(length, HEAD_DIM)
     else:
+        query_t = dot32(own_part(every), weights[0]).astype(jnp.bfloat16)
+        key_t, value_t = project(every, weights[1:3])
+        seed_queries = dot32(own_part(seed_normed), weights[3]).astype(jnp.bfloat16)
+        key_s, value_s = project(chosen, weights[4:])
         target_mixed = attend(query_t, key_t, value_t)
         student_mixed = attend(seed_queries, key_s, value_s)
         both = jnp.concatenate([target_mixed, student_mixed], axis=1)

time: 143 us -> 134 us (0.937)
  Pallas kernels: 88.3 us -> 82.3 us
  matrix products: 7.33 us -> 2.71 us
  waiting for transfers between devices: 4.37 us -> 6.22 us
  local copies, waits for them, and re-layouts: 8.12 us -> 6.31 us
    pallas_call x2, Pallas kernels: 63.3 us -> 49.1 us  [gather_rows(): pl.pallas_call(functools.partial(gather_kernel, shards, with_seeds), out_...]
    pallas_call x1, Pallas kernels: 24.9 us -> 33.2 us  [middle(): pl.pallas_call(functools.partial(middle_kernel, shards), out_shape=[jax.S...]
    dot_general x3 -> x0, matrix products: 5.32 us -> none  [the longest x1 3.04 us: dot32(): return jnp.dot(left, right, preferred_element_type=jnp.float32)]
    convert_element_type x3 -> x0, local copies, waits for them, and re-layouts: 2.5 us -> none  [the longest x2 2.33 us: project(): return jnp.einsum('nr,krc->knc', rows, some, preferred_element_type=jnp.f...]
    ppermute x2, waiting for transfers between devices: 0.01 us -> 1.87 us  [both_of_dp(): other = lax.ppermute(block, 'dp', [(0, 1), (1, 0)])]
    concatenate x0 -> x1, other arithmetic: none -> 1.76 us  [both_of_dp(): jnp.concatenate([jnp.where(first, block, other), jnp.where(first, other,...]
    ppermute x0 -> x1, local copies, waits for them, and re-layouts: none -> 1.6 us  [both_of_dp(): other = lax.ppermute(block, 'dp', [(0, 1), (1, 0)])]
  transfers between devices with their start and end apart: 3 -> 3, of which waited for: 1 -> 2; matrix products, arithmetic and copies ran while one was open for 11% -> 9% of each run, Pallas kernels for 24% -> 21%
where the time goes in v4:
time: 134 us
  Pallas kernels  82.3 us (61%)
  blocking collectives  16.5 us (12%)
  other arithmetic  14.4 us (11%)
  local copies, waits for them, and re-layouts  6.31 us (5%)
  waiting for transfers between devices  6.22 us (5%)
  starting transfers between devices  4.55 us (3%)
  matrix products  2.71 us (2%)
    pallas_call x2, Pallas kernels, gather_rows(): pl.pallas_call(functools.partial(gather_kernel, shards, with_seeds), out_...  49.1 us
    pallas_call x1, Pallas kernels, middle(): pl.pallas_call(functools.partial(middle_kernel, shards), out_shape=[jax.S...  33.2 us
    all_gather x1, blocking collectives, body(): lax.all_gather(head_grad, 'seq', axis=0, tiled=True).astype(jnp.float32)  16.5 us
    ppermute x1, waiting for transfers between devices, body(): came = lax.ppermute(send, 'dp', [(0, 1), (1, 0)])  4.35 us
    select_n x2, other arithmetic, both_of_dp(): jnp.where(first, block, other)  3.2 us
    add x1, other arithmetic, body(): MOMENTUM * target_out.astype(jnp.float32)  3.2 us
    ppermute x2, starting transfers between devices, both_of_dp(): other = lax.ppermute(block, 'dp', [(0, 1), (1, 0)])  2.99 us
  transfers between devices with their start and end apart: 3, of which 2 were waited for; matrix products, arithmetic and copies ran while one was open for 9% of the time, Pallas kernels for 21%

profile of v4, /device:TPU:0, one launch (start us, length us, event | category | flops | bytes accessed | tf_op | source)
XLA Modules:
  0.0 133.9 jit_solution(17508613565564002381)
XLA Ops:
  0.6 2.0 %constant_dynamic-slice_fusion = (bf16[3,704,88]{2,1,0:T(8,128)(2,1)S(1)}, bf16[3,704,88]{2,1,0:T(8,128)(2,1)S(1)}) fusion(bf16[3,704,704]{2,1,0:T(8,128)(2,1)} %param.13, s32[]{:T(128)S(6)} %select_n.57, bf16[3,704,704]{2,1,0:T(8,128)(2,1)} %param.11), kind=kLoop, calls=%fused_computation.44 | loop fusion | bytes 1486852 | tf_op jit(solution)/shard_map/dynamic_slice | solution.py:441
  2.6 0.8 copy-done.4
  3.9 1.3 copy.15
  5.2 3.0 %collective-permute-start = (bf16[6,704,88]{1,2,0:T(8,128)(2,1)}, bf16[6,704,88]{1,2,0:T(8,128)(2,1)}, u32[]{:S(2)}, u32[]{:S(2)}) collective-permute-start(bf16[6,704,88]{1,2,0:T(8,128)(2,1)} %copy.15), channel_id=1, source_target_pairs={{0,1},{1,0},{2,3},{3,2},{4,5},{5,4},{6,7},{7,6},{8,9},{9,8},{10,11... | collective-permute-start | bytes 2230280 | tf_op jit(solution)/shard_map/ppermute | solution.py:420
  8.3 0.2 multiply_reduce_fusion
  8.7 0.8 convert_bitcast_fusion
  9.6 0.8 multiply_sine_fusion
  10.8 27.9 %gather_seeds.1 = (bf16[8,2,2,32,1408]{4,3,2,1,0:T(8,128)(2,1)S(1)}, s32[8,8,384]{2,1,0:T(8,128)S(1)}, bf16[1024,1408]{1,0:T(8,128)(2,1)}) custom-call(bf16[2,32,1408]{2,1,0:T(8,128)(2,1)S(1)} %multiply_convert_fusion.refs_0_, s32[8,384]{1,0:T(8,128)S(1)} %pad.4.refs_1_, f32[32,1408]{1,0:T(8,128)S(1)} %get-tuple-element.25.refs_2_, ...), custom_call_target="tpu_custom_call" | custom-call | tf_op jit(solution)/shard_map/gather_seeds/pallas_call | solution.py:249
  38.7 0.7 fusion.7
  39.6 1.0 reduce_window_sum.11
  40.9 2.1 %convolution_convert_fusion = bf16[8,32,1408]{2,1,0:T(8,128)(2,1)} fusion(bf16[8,128,1408]{2,1,0:T(8,128)(2,1)S(1)} %bitcast.23, s32[8,128]{1,0:T(8,128)S(1)} %broadcast_add_fusion, pred[8,128]{1,0:T(8,128)(4,1)} %get-tuple-element.15), kind=kOutput, calls=%fused_computation.1 | convolution fusion | flops 92700672 | bytes 3609600 | tf_op jit(solution)/shard_map/sck,skw->scw/dot_general | solution.py:476
  43.0 1.6 %copy.16 = bf16[6,704,88]{2,1,0:T(8,128)(2,1)S(1)} copy(bf16[6,704,88]{1,2,0:T(8,128)(2,1)} %collective-permute-done) | data formatting | bytes 1486848 | tf_op jit(solution)/shard_map/ppermute | solution.py:420
  44.6 1.5 %broadcast_select_fusion.3 = (bf16[6,704,88]{2,1,0:T(8,128)(2,1)S(1)}, bf16[6,704,88]{2,1,0:T(8,128)(2,1)S(1)}) fusion(bf16[6,704,88]{2,1,0:T(8,128)(2,1)S(1)} %copy.16, pred[]{:T(512)S(6)} %eq.36, bf16[3,704,88]{2,1,0:T(8,128)(2,1)} %copy-done.4, bf16[3,704,88]{2,1,0:T(8,128)(2,1)} %copy-done.5), kind=kLoop, calls=%fused_computation.9 | loop fusion | flops 1115136 | bytes 2973697 | tf_op jit(solution)/shard_map/jit(_where)/select_n | solution.py:423
  46.1 1.8 %pad_maximum_fusion.refs_3_ = bf16[6,1408,88]{2,1,0:T(8,128)(2,1)} fusion(bf16[6,704,88]{2,1,0:T(8,128)(2,1)S(1)} %get-tuple-element.19, bf16[6,704,88]{2,1,0:T(8,128)(2,1)S(1)} %get-tuple-element.18), kind=kLoop, calls=%fused_computation.3 | loop fusion | flops 2973696 | bytes 2973696 | tf_op jit(solution)/shard_map/concatenate | solution.py:422
  47.9 1.9 %collective-permute-done.1 = bf16[704,704]{1,0:T(8,128)(2,1)} collective-permute-done((bf16[704,704]{1,0:T(8,128)(2,1)}, bf16[704,704]{1,0:T(8,128)(2,1)}, u32[]{:S(2)}, u32[]{:S(2)}) %collective-permute-start.1) | collective-permute-done | bytes 991264 | tf_op jit(solution)/shard_map/ppermute | solution.py:420
  49.7 1.7 %broadcast_select_fusion.1 = (bf16[704,704]{1,0:T(8,128)(2,1)S(1)}, bf16[704,704]{1,0:T(8,128)(2,1)S(1)}) fusion(bf16[704,704]{1,0:T(8,128)(2,1)} %param.14, bf16[704,704]{1,0:T(8,128)(2,1)} %collective-permute-done.1, pred[]{:T(512)S(6)} %eq.36), kind=kLoop, calls=%fused_computation.7 | loop fusion | flops 991232 | bytes 3964929 | tf_op jit(solution)/shard_map/jit(_where)/select_n | solution.py:423
  51.5 3.2 %multiply_add_fusion = (f32[704,1408]{1,0:T(8,128)}, bf16[704,1408]{1,0:T(8,128)(2,1)S(1)}) fusion(bf16[704,1408]{1,0:T(8,128)(2,1)S(1)} %copy-done.1, bf16[704,704]{1,0:T(8,128)(2,1)S(1)} %get-tuple-element.17, bf16[704,704]{1,0:T(8,128)(2,1)S(1)} %get-tuple-element.16), kind=kLoop, calls=%fused_computation | loop fusion | flops 8921088 | bytes 9912320 | tf_op jit(solution)/shard_map/add | solution.py:556
  54.7 33.2 %middle.1 = (bf16[64,1408]{1,0:T(8,128)(2,1)S(1)}, bf16[8,128,88]{2,1,0:T(8,128)(2,1)S(1)}) custom-call(bf16[8,128,1408]{2,1,0:T(8,128)(2,1)} %bitcast.24, bf16[8,128,1408]{2,1,0:T(8,128)(2,1)} %bitcast.28, bf16[256,1408]{1,0:T(8,128)(2,1)S(1)} %bitcast.25, bf16[6,1408,88]{2,1,0:T(8,128)(2,1)} %pad_maximum_fusion.refs_3_, bf16[704,1408]{1,0:T(8,128)(2,1)S(1)} %copy-done.1, ...), custom_call_target="tpu_custom_call" | custom-call | tf_op jit(solution)/shard_map/middle/pallas_call | solution.py:372
  87.9 21.2 %gather_rows.1 = bf16[8,2,2,32,1408]{4,3,2,1,0:T(8,128)(2,1)S(1)} custom-call(bf16[2,32,1408]{2,1,0:T(8,128)(2,1)S(1)} %bitcast.27), custom_call_target="tpu_custom_call" | custom-call | tf_op jit(solution)/shard_map/gather_rows/pallas_call | solution.py:249
  109.2 0.6 convolution_convert_fusion.1
  109.9 1.6 %collective-permute-start.2 = (bf16[88,704]{1,0:T(8,128)(2,1)S(1)}, bf16[88,704]{1,0:T(8,128)(2,1)S(1)}, u32[]{:S(2)}, u32[]{:S(2)}) collective-permute-start(bf16[88,704]{1,0:T(8,128)(2,1)S(1)} %broadcast_select_fusion.4), channel_id=1, source_target_pairs={{0,1},{1,0},{2,3},{3,2},{4,5},{5,4},{6,7},{7,6},{8,9},{9,8},{10,11... | collective-permute-start | bytes 371720 | tf_op jit(solution)/shard_map/ppermute | solution.py:548
  111.4 4.4 %collective-permute-done.2 = bf16[88,704]{1,0:T(8,128)(2,1)S(1)} collective-permute-done((bf16[88,704]{1,0:T(8,128)(2,1)S(1)}, bf16[88,704]{1,0:T(8,128)(2,1)S(1)}, u32[]{:S(2)}, u32[]{:S(2)}) %collective-permute-start.2) | collective-permute-done | bytes 123936 | tf_op jit(solution)/shard_map/ppermute | solution.py:548
  115.9 16.5 %all_gather.3 = bf16[704,704]{1,0:T(8,128)(2,1)S(1)} all-gather(bf16[88,704]{1,0:T(8,128)(2,1)S(1)} %add_convert_fusion), channel_id=1, replica_groups=mesh['seq'=8,'grp'=2,'dp'=2] {'seq'}, dimensions={0}, use_global_device_ids=true | all-gather | bytes 1115136 | tf_op jit(solution)/shard_map/all_gather | solution.py:552
  132.4 1.5 %convert_element_type.84 = f32[704,704]{1,0:T(8,128)} convert(bf16[704,704]{1,0:T(8,128)(2,1)S(1)} %all_gather.3) | non-fusion elementwise | flops 495616 | bytes 2973696 | tf_op jit(solution)/shard_map/convert_element_type | solution.py:552
  (50 shorter events, 2.0 us)
Async XLA Ops:
  2.6 0.8 copy-start.4
  2.6 1.0 copy-start.5
  3.6 4.6 %copy-start.6 = (bf16[1,128,1408]{2,1,0:T(8,128)(2,1)S(1)}, bf16[1,128,1408]{2,1,0:T(8,128)(2,1)}, u32[]{:S(2)}) copy-start(bf16[1,128,1408]{2,1,0:T(8,128)(2,1)} %param.8) | copy-start | bytes 1081348
  3.9 5.7 %copy-start.8 = (s32[1,192]{1,0:T(1,128)S(1)}, s32[1,192]{1,0:T(1,128)}, u32[]{:S(2)}) copy-start(s32[1,192]{1,0:T(1,128)} %param.10) | copy-start | bytes 2308
  3.9 5.7 %copy-start.9 = (s32[1,128]{1,0:T(1,128)S(1)}, s32[1,128]{1,0:T(1,128)}, u32[]{:S(2)}) copy-start(s32[1,128]{1,0:T(1,128)} %param.9) | copy-start | bytes 1540
  3.9 5.7 %copy-start.7 = (f32[1408]{0:T(1024)S(1)}, f32[1408]{0:T(1024)}, u32[]{:S(2)}) copy-start(f32[1408]{0:T(1024)} %param.15) | copy-start | bytes 16900
  5.2 37.8 %collective-permute-start = (bf16[6,704,88]{1,2,0:T(8,128)(2,1)}, bf16[6,704,88]{1,2,0:T(8,128)(2,1)}, u32[]{:S(2)}, u32[]{:S(2)}) collective-permute-start(bf16[6,704,88]{1,2,0:T(8,128)(2,1)} %copy.15), channel_id=1, source_target_pairs={{0,1},{1,0},{2,3},{3,2},{4,5},{5,4},{6,7},{7,6},{8,9},{9,8},{10,11... | collective-permute-start | bytes 2230280 | tf_op jit(solution)/shard_map/ppermute | solution.py:420
  8.2 41.6 %collective-permute-start.1 = (bf16[704,704]{1,0:T(8,128)(2,1)}, bf16[704,704]{1,0:T(8,128)(2,1)}, u32[]{:S(2)}, u32[]{:S(2)}) collective-permute-start(bf16[704,704]{1,0:T(8,128)(2,1)} %param.14), channel_id=1, source_target_pairs={{0,1},{1,0},{2,3},{3,2},{4,5},{5,4},{6,7},{7,6},{8,9},{9,8},{10,11... | collective-permute-start | bytes 2973704 | tf_op jit(solution)/shard_map/ppermute | solution.py:420
  38.6 4.4 %copy-start = (bf16[8,2,2,32,1408]{4,3,2,1,0:T(8,128)(2,1)}, bf16[8,2,2,32,1408]{4,3,2,1,0:T(8,128)(2,1)S(1)}, u32[]{:S(2)}) copy-start(bf16[8,2,2,32,1408]{4,3,2,1,0:T(8,128)(2,1)S(1)} %get-tuple-element.7) | copy-start | bytes 8650756
  47.9 3.6 %copy-start.1 = (bf16[704,1408]{1,0:T(8,128)(2,1)S(1)}, bf16[704,1408]{1,0:T(8,128)(2,1)}, u32[]{:S(2)}) copy-start(bf16[704,1408]{1,0:T(8,128)(2,1)} %refs_4_.1) | copy-start | bytes 5947396
  51.4 3.2 %copy-start.2 = (bf16[8,32,1408]{2,1,0:T(8,128)(2,1)S(1)}, bf16[8,32,1408]{2,1,0:T(8,128)(2,1)}, u32[]{:S(2)}) copy-start(bf16[8,32,1408]{2,1,0:T(8,128)(2,1)} %convolution_convert_fusion) | copy-start | bytes 2162692
  51.5 3.2 %copy-start.3 = (f32[64,1408]{1,0:T(8,128)S(1)}, f32[64,1408]{1,0:T(8,128)}, u32[]{:S(2)}) copy-start(f32[64,1408]{1,0:T(8,128)} %get-tuple-element.20.refs_6_) | copy-start | bytes 1081348
  109.9 5.9 %collective-permute-start.2 = (bf16[88,704]{1,0:T(8,128)(2,1)S(1)}, bf16[88,704]{1,0:T(8,128)(2,1)S(1)}, u32[]{:S(2)}, u32[]{:S(2)}) collective-permute-start(bf16[88,704]{1,0:T(8,128)(2,1)S(1)} %broadcast_select_fusion.4), channel_id=1, source_target_pairs={{0,1},{1,0},{2,3},{3,2},{4,5},{5,4},{6,7},{7,6},{8,9},{9,8},{10,11... | collective-permute-start | bytes 371720 | tf_op jit(solution)/shard_map/ppermute | solution.py:548

commit v5 on v4

--- a/solution.py
+++ b/solution.py
@@ -264,7 +264,7 @@
 
 def middle_kernel(shards, *refs):
     (
-        every, seeded, chosen, weights, out_t, out_s, tokens_ref, seeds_ref, usable_ref,
+        every, seeded, chosen, weights, out_t, own_s, other_s, tokens_ref, seeds_ref, usable_ref,
         back_ref, mix_s, k_t, v_t, k_s, v_s, mix_t, got_t, got_s, part_t, part_s, came_t, came_s,
         send_t, recv_t, send_s, recv_s, y_send, y_recv,
     ) = refs
@@ -319,9 +319,11 @@
             device_id_type=MESH,
         )
 
-    def project(got, weights, part):
-        rows = jnp.concatenate([got[k] for k in range(shards)], axis=1)
-        whole = dot32(rows, weights[...]).astype(jnp.bfloat16)
+    def joined(got):
+        return jnp.concatenate([got[k] for k in range(shards)], axis=1)
+
+    def place(columns, part):
+        whole = jnp.concatenate(columns, axis=1).astype(jnp.bfloat16)
         half = whole.shape[0] // 2
         part[0] = whole[:half]
         part[1] = whole[half:]
@@ -342,12 +344,23 @@
     heads(seeded, 3, k_s, v_s, mix_s, got_s, send_s, recv_s)
     for k in range(shards - 1):
         copy(k, mix_t, got_t, send_t, recv_t).wait_recv()
-    project(got_t, out_t, part_t)
+    place([dot32(joined(got_t), out_t[...])], part_t)
     copy(0, mix_s, got_s, send_s, recv_s).wait_recv()
     y_copy(0, part_t, came_t).start()
     for k in range(1, shards - 1):
         copy(k, mix_s, got_s, send_s, recv_s).wait_recv()
-    project(got_s, out_s, part_s)
+    rows = joined(got_s)
+    own_columns, other_columns = dot32(rows, own_s[...]), dot32(rows, other_s[...])
+    first = lax.axis_index("dp") == 0
+
+    @pl.when(first)
+    def _():
+        place([own_columns, other_columns], part_s)
+
+    @pl.when(jnp.logical_not(first))
+    def _():
+        place([other_columns, own_columns], part_s)
+
     y_copy(0, part_t, came_t).wait_recv()
     y_copy(1, part_s, came_s).start()
     tokens = tokens_ref[...].astype(jnp.float32)
@@ -366,7 +379,7 @@
     blocked = operands[0].shape[:2] + (HEAD_DIM,)
     flat = (blocked[0] * blocked[1], HEAD_DIM)
     some = (operands[2].shape[0], HEAD_DIM)
-    rows, width = operands[6].shape
+    rows, width = operands[7].shape
     bf16, dma = jnp.bfloat16, pltpu.SemaphoreType.DMA
     vmem = pl.BlockSpec(memory_space=pltpu.VMEM)
     return pl.pallas_call(
@@ -414,10 +427,15 @@
     return jnp.dot(left, right, preferred_element_type=jnp.float32)
 
 
-def both_of_dp(block, axis):
+def swap(block):
+    return lax.ppermute(block, "dp", [(0, 1), (1, 0)])
+
+
+def both_of_dp(block, axis, other=None):
     if lax.axis_size("dp") != 2:
         return lax.all_gather(block, "dp", axis=axis, tiled=True)
-    other = lax.ppermute(block, "dp", [(0, 1), (1, 0)])
+    if other is None:
+        other = swap(block)
     first = lax.axis_index("dp") == 0
     return jnp.concatenate(
         [jnp.where(first, block, other), jnp.where(first, other, block)], axis=axis
@@ -442,7 +460,11 @@
 
     mine = jnp.concatenate([columns(target_qkv), columns(student_qkv)], axis=0)
     weights = both_of_dp(mine, 1)
-    relaid = both_of_dp(student_out, 1)
+    fused = rep == 1 and lax.axis_size("dp") == 2
+    if fused:
+        other_out = swap(student_out)
+    else:
+        relaid = both_of_dp(student_out, 1)
 
     grp = lax.axis_index("grp")
     half_rows = row_count // 2
@@ -492,13 +514,13 @@
     usable = jnp.sum(
         (lists[None, :] == places[:, None]).astype(jnp.float32), axis=1, keepdims=True
     )
-    if rep == 1:
+    if fused:
         blocked = (shards, row_count, width)
         back_grad, student_mixed = middle(
             shards,
             [
                 every.reshape(blocked), seed_normed.reshape(blocked), chosen, weights,
-                target_out, relaid, own_tokens, own_seeds, usable,
+                target_out, student_out, other_out, own_tokens, own_seeds, usable,
             ],
         )
         student_mixed = student_mixed.reshape(length, HEAD_DIM)
@@ -540,6 +562,11 @@
         (((0,), (0,)), ((), ())),
         preferred_element_type=jnp.float32,
     ).astype(jnp.bfloat16)
+    if fused:
+        head_grad, target_out, student_out, other_out = lax.optimization_barrier(
+            (head_grad, target_out, student_out, other_out)
+        )
+        relaid = both_of_dp(student_out, 1, other_out)
     if lax.axis_size("dp") == 2:
         half = head_grad.shape[1] // 2
         first = lax.axis_index("dp") == 0

time: 134 us -> 131 us (0.978)
  waiting for transfers between devices: 6.22 us -> 1.81 us
    ppermute x1, waiting for transfers between devices: 4.35 us -> 0.01 us  [body(): came = lax.ppermute(send, 'dp', [(0, 1), (1, 0)])]
  transfers between devices with their start and end apart: 3 -> 3, of which waited for: 2 -> 1; matrix products, arithmetic and copies ran while one was open for 9% -> 13% of each run, Pallas kernels for 21% -> 21%
where the time goes in v5:
time: 131 us
  Pallas kernels  83 us (63%)
  blocking collectives  17.2 us (13%)
  other arithmetic  14.3 us (11%)
  local copies, waits for them, and re-layouts  6.27 us (5%)
  starting transfers between devices  4.55 us (3%)
  matrix products  2.71 us (2%)
  waiting for transfers between devices  1.81 us (1%)
    pallas_call x2, Pallas kernels, gather_rows(): pl.pallas_call(functools.partial(gather_kernel, shards, with_seeds), out_...  49.1 us
    pallas_call x1, Pallas kernels, middle(): pl.pallas_call(functools.partial(middle_kernel, shards), out_shape=[jax.S...  33.9 us
    all_gather x1, blocking collectives, body(): lax.all_gather(head_grad, 'seq', axis=0, tiled=True).astype(jnp.float32)  17.2 us
    select_n x2, other arithmetic, both_of_dp(): jnp.where(first, block, other)  3.24 us
    add x1, other arithmetic, body(): MOMENTUM * target_out.astype(jnp.float32)  3.02 us
    ppermute x2, starting transfers between devices, swap(): return lax.ppermute(block, 'dp', [(0, 1), (1, 0)])  2.99 us
  transfers between devices with their start and end apart: 3, of which 1 were waited for; matrix products, arithmetic and copies ran while one was open for 13% of the time, Pallas kernels for 21%

profile of v5, /device:TPU:0, one launch (start us, length us, event | category | flops | bytes accessed | tf_op | source)
XLA Modules:
  0.0 130.7 jit_solution(15599541075170579305)
XLA Ops:
  0.6 2.0 %constant_dynamic-slice_fusion = (bf16[3,704,88]{2,1,0:T(8,128)(2,1)S(1)}, bf16[3,704,88]{2,1,0:T(8,128)(2,1)S(1)}) fusion(bf16[3,704,704]{2,1,0:T(8,128)(2,1)} %param.13, s32[]{:T(128)S(6)} %select_n.57, bf16[3,704,704]{2,1,0:T(8,128)(2,1)} %param.11), kind=kLoop, calls=%fused_computation.43 | loop fusion | bytes 1486852 | tf_op jit(solution)/shard_map/dynamic_slice | solution.py:459
  2.7 0.8 copy-done.4
  3.6 0.2 pad_maximum_fusion.1
  3.8 1.3 %copy.15 = bf16[6,704,88]{1,2,0:T(8,128)(2,1)} copy(bf16[6,704,88]{2,1,0:T(8,128)(2,1)S(1)} %pad_maximum_fusion.1) | data formatting | bytes 1486848 | tf_op jit(solution)/shard_map/concatenate | solution.py:461
  5.2 3.0 %collective-permute-start = (bf16[6,704,88]{1,2,0:T(8,128)(2,1)}, bf16[6,704,88]{1,2,0:T(8,128)(2,1)}, u32[]{:S(2)}, u32[]{:S(2)}) collective-permute-start(bf16[6,704,88]{1,2,0:T(8,128)(2,1)} %copy.15), channel_id=1, source_target_pairs={{0,1},{1,0},{2,3},{3,2},{4,5},{5,4},{6,7},{7,6},{8,9},{9,8},{10,11... | collective-permute-start | bytes 2230280 | tf_op jit(solution)/shard_map/ppermute | solution.py:431
  8.3 0.2 multiply_reduce_fusion
  8.6 0.8 convert_bitcast_fusion
  9.6 0.8 multiply_sine_fusion
  10.7 27.9 %gather_seeds.1 = (bf16[8,2,2,32,1408]{4,3,2,1,0:T(8,128)(2,1)S(1)}, s32[8,8,384]{2,1,0:T(8,128)S(1)}, bf16[1024,1408]{1,0:T(8,128)(2,1)}) custom-call(bf16[2,32,1408]{2,1,0:T(8,128)(2,1)S(1)} %multiply_convert_fusion.refs_0_, s32[8,384]{1,0:T(8,128)S(1)} %pad.4.refs_1_, f32[32,1408]{1,0:T(8,128)S(1)} %get-tuple-element.31.refs_2_, ...), custom_call_target="tpu_custom_call" | custom-call | tf_op jit(solution)/shard_map/gather_seeds/pallas_call | solution.py:249
  38.6 0.7 fusion.7
  39.6 1.0 reduce_window_sum.11
  40.8 2.1 %convolution_convert_fusion = bf16[8,32,1408]{2,1,0:T(8,128)(2,1)} fusion(bf16[8,128,1408]{2,1,0:T(8,128)(2,1)S(1)} %bitcast.22, s32[8,128]{1,0:T(8,128)S(1)} %broadcast_add_fusion, pred[8,128]{1,0:T(8,128)(4,1)} %get-tuple-element.21), kind=kOutput, calls=%fused_computation.1 | convolution fusion | flops 92700672 | bytes 3609600 | tf_op jit(solution)/shard_map/sck,skw->scw/dot_general | solution.py:498
  42.9 1.6 %copy.16 = bf16[6,704,88]{2,1,0:T(8,128)(2,1)S(1)} copy(bf16[6,704,88]{1,2,0:T(8,128)(2,1)} %collective-permute-done) | data formatting | bytes 1486848 | tf_op jit(solution)/shard_map/ppermute | solution.py:431
  44.5 1.5 %broadcast_select_fusion.3 = (bf16[6,704,88]{2,1,0:T(8,128)(2,1)S(1)}, bf16[6,704,88]{2,1,0:T(8,128)(2,1)S(1)}) fusion(bf16[6,704,88]{2,1,0:T(8,128)(2,1)S(1)} %copy.16, pred[]{:T(512)S(6)} %eq.36, bf16[3,704,88]{2,1,0:T(8,128)(2,1)} %copy-done.4, bf16[3,704,88]{2,1,0:T(8,128)(2,1)} %copy-done.5), kind=kLoop, calls=%fused_computation.8 | loop fusion | flops 1115136 | bytes 2973697 | tf_op jit(solution)/shard_map/jit(_where)/select_n | solution.py:441
  46.1 1.8 %pad_maximum_fusion.refs_3_ = bf16[6,1408,88]{2,1,0:T(8,128)(2,1)} fusion(bf16[6,704,88]{2,1,0:T(8,128)(2,1)S(1)} %get-tuple-element.25, bf16[6,704,88]{2,1,0:T(8,128)(2,1)S(1)} %get-tuple-element.24), kind=kLoop, calls=%fused_computation.3 | loop fusion | flops 2973696 | bytes 2973696 | tf_op jit(solution)/shard_map/concatenate | solution.py:440
  47.9 1.8 %collective-permute-done.1.refs_6_ = bf16[704,704]{1,0:T(8,128)(2,1)} collective-permute-done((bf16[704,704]{1,0:T(8,128)(2,1)}, bf16[704,704]{1,0:T(8,128)(2,1)}, u32[]{:S(2)}, u32[]{:S(2)}) %collective-permute-start.1) | collective-permute-done | bytes 991264 | tf_op jit(solution)/shard_map/ppermute | solution.py:431
  49.7 33.9 %middle.1 = (bf16[64,1408]{1,0:T(8,128)(2,1)S(1)}, bf16[8,128,88]{2,1,0:T(8,128)(2,1)S(1)}) custom-call(bf16[8,128,1408]{2,1,0:T(8,128)(2,1)} %bitcast.23, bf16[8,128,1408]{2,1,0:T(8,128)(2,1)} %bitcast.28, bf16[256,1408]{1,0:T(8,128)(2,1)S(1)} %bitcast.25, bf16[6,1408,88]{2,1,0:T(8,128)(2,1)} %pad_maximum_fusion.refs_3_, bf16[704,1408]{1,0:T(8,128)(2,1)S(1)} %copy-done.1, ...), custom_call_target="tpu_custom_call" | custom-call | tf_op jit(solution)/shard_map/middle/pallas_call | solution.py:385
  83.6 21.2 %gather_rows.1 = bf16[8,2,2,32,1408]{4,3,2,1,0:T(8,128)(2,1)S(1)} custom-call(bf16[2,32,1408]{2,1,0:T(8,128)(2,1)S(1)} %bitcast.27), custom_call_target="tpu_custom_call" | custom-call | tf_op jit(solution)/shard_map/gather_rows/pallas_call | solution.py:249
  104.9 0.6 convolution_convert_fusion.1
  105.6 1.6 %collective-permute-start.2 = (bf16[88,704]{1,0:T(8,128)(2,1)S(1)}, bf16[88,704]{1,0:T(8,128)(2,1)S(1)}, u32[]{:S(2)}, u32[]{:S(2)}) collective-permute-start(bf16[88,704]{1,0:T(8,128)(2,1)S(1)} %broadcast_select_fusion.4), channel_id=1, source_target_pairs={{0,1},{1,0},{2,3},{3,2},{4,5},{5,4},{6,7},{7,6},{8,9},{9,8},{10,11... | collective-permute-start | bytes 371720 | tf_op jit(solution)/shard_map/ppermute | solution.py:575
  107.1 1.7 %broadcast_select_fusion.1 = (bf16[704,704]{1,0:T(8,128)(2,1)S(1)}, bf16[704,704]{1,0:T(8,128)(2,1)S(1)}) fusion(bf16[704,704]{1,0:T(8,128)(2,1)} %refs_5_.1, bf16[704,704]{1,0:T(8,128)(2,1)} %collective-permute-done.1.refs_6_, pred[]{:T(512)S(6)} %eq.36), kind=kLoop, calls=%fused_computation.6 | loop fusion | flops 991232 | bytes 3964929 | tf_op jit(solution)/shard_map/jit(_where)/select_n | solution.py:441
  108.8 3.0 %multiply_add_fusion = f32[704,1408]{1,0:T(8,128)} fusion(bf16[704,1408]{1,0:T(8,128)(2,1)S(1)} %copy-done.1, bf16[704,704]{1,0:T(8,128)(2,1)S(1)} %get-tuple-element.23, bf16[704,704]{1,0:T(8,128)(2,1)S(1)} %get-tuple-element.22), kind=kLoop, calls=%fused_computation | loop fusion | flops 7929856 | bytes 7929856 | tf_op jit(solution)/shard_map/add | solution.py:583
  112.0 17.2 %all_gather.3 = bf16[704,704]{1,0:T(8,128)(2,1)S(1)} all-gather(bf16[88,704]{1,0:T(8,128)(2,1)S(1)} %add_convert_fusion), channel_id=1, replica_groups=mesh['seq'=8,'grp'=2,'dp'=2] {'seq'}, dimensions={0}, use_global_device_ids=true | all-gather | bytes 1115136 | tf_op jit(solution)/shard_map/all_gather | solution.py:579
  129.2 1.5 %convert_element_type.84 = f32[704,704]{1,0:T(8,128)} convert(bf16[704,704]{1,0:T(8,128)(2,1)S(1)} %all_gather.3) | non-fusion elementwise | flops 495616 | bytes 2973696 | tf_op jit(solution)/shard_map/convert_element_type | solution.py:579
  (50 shorter events, 1.7 us)
Async XLA Ops:
  2.6 0.8 copy-start.4
  2.6 1.0 copy-start.5
  2.6 5.5 %copy-start.6 = (bf16[1,128,1408]{2,1,0:T(8,128)(2,1)S(1)}, bf16[1,128,1408]{2,1,0:T(8,128)(2,1)}, u32[]{:S(2)}) copy-start(bf16[1,128,1408]{2,1,0:T(8,128)(2,1)} %param.8) | copy-start | bytes 1081348
  3.6 5.9 %copy-start.8 = (s32[1,192]{1,0:T(1,128)S(1)}, s32[1,192]{1,0:T(1,128)}, u32[]{:S(2)}) copy-start(s32[1,192]{1,0:T(1,128)} %param.10) | copy-start | bytes 2308
  3.6 5.9 %copy-start.9 = (s32[1,128]{1,0:T(1,128)S(1)}, s32[1,128]{1,0:T(1,128)}, u32[]{:S(2)}) copy-start(s32[1,128]{1,0:T(1,128)} %param.9) | copy-start | bytes 1540
  3.6 5.9 %copy-start.7 = (f32[1408]{0:T(1024)S(1)}, f32[1408]{0:T(1024)}, u32[]{:S(2)}) copy-start(f32[1408]{0:T(1024)} %param.15) | copy-start | bytes 16900
  5.2 37.8 %collective-permute-start = (bf16[6,704,88]{1,2,0:T(8,128)(2,1)}, bf16[6,704,88]{1,2,0:T(8,128)(2,1)}, u32[]{:S(2)}, u32[]{:S(2)}) collective-permute-start(bf16[6,704,88]{1,2,0:T(8,128)(2,1)} %copy.15), channel_id=1, source_target_pairs={{0,1},{1,0},{2,3},{3,2},{4,5},{5,4},{6,7},{7,6},{8,9},{9,8},{10,11... | collective-permute-start | bytes 2230280 | tf_op jit(solution)/shard_map/ppermute | solution.py:431
  8.1 41.6 %collective-permute-start.1 = (bf16[704,704]{1,0:T(8,128)(2,1)}, bf16[704,704]{1,0:T(8,128)(2,1)}, u32[]{:S(2)}, u32[]{:S(2)}) collective-permute-start(bf16[704,704]{1,0:T(8,128)(2,1)} %refs_5_.1), channel_id=1, source_target_pairs={{0,1},{1,0},{2,3},{3,2},{4,5},{5,4},{6,7},{7,6},{8,9},{9,8},{10,11... | collective-permute-start | bytes 2973704 | tf_op jit(solution)/shard_map/ppermute | solution.py:431
  38.6 4.4 %copy-start = (bf16[8,2,2,32,1408]{4,3,2,1,0:T(8,128)(2,1)}, bf16[8,2,2,32,1408]{4,3,2,1,0:T(8,128)(2,1)S(1)}, u32[]{:S(2)}) copy-start(bf16[8,2,2,32,1408]{4,3,2,1,0:T(8,128)(2,1)S(1)} %get-tuple-element.11) | copy-start | bytes 8650756
  46.1 3.6 %copy-start.1 = (bf16[704,1408]{1,0:T(8,128)(2,1)S(1)}, bf16[704,1408]{1,0:T(8,128)(2,1)}, u32[]{:S(2)}) copy-start(bf16[704,1408]{1,0:T(8,128)(2,1)} %refs_4_.1) | copy-start | bytes 5947396
  46.1 3.6 %copy-start.2 = (bf16[8,32,1408]{2,1,0:T(8,128)(2,1)S(1)}, bf16[8,32,1408]{2,1,0:T(8,128)(2,1)}, u32[]{:S(2)}) copy-start(bf16[8,32,1408]{2,1,0:T(8,128)(2,1)} %convolution_convert_fusion) | copy-start | bytes 2162692
  46.1 3.6 %copy-start.3 = (f32[64,1408]{1,0:T(8,128)S(1)}, f32[64,1408]{1,0:T(8,128)}, u32[]{:S(2)}) copy-start(f32[64,1408]{1,0:T(8,128)} %get-tuple-element.26.refs_7_) | copy-start | bytes 1081348
  105.6 6.3 %collective-permute-start.2 = (bf16[88,704]{1,0:T(8,128)(2,1)S(1)}, bf16[88,704]{1,0:T(8,128)(2,1)S(1)}, u32[]{:S(2)}, u32[]{:S(2)}) collective-permute-start(bf16[88,704]{1,0:T(8,128)(2,1)S(1)} %broadcast_select_fusion.4), channel_id=1, source_target_pairs={{0,1},{1,0},{2,3},{3,2},{4,5},{5,4},{6,7},{7,6},{8,9},{9,8},{10,11... | collective-permute-start | bytes 371720 | tf_op jit(solution)/shard_map/ppermute | solution.py:575

commit v6 on v5

--- a/solution.py
+++ b/solution.py
@@ -9,7 +9,7 @@
 from jax.sharding import PartitionSpec as P
 
 MESH = pl.DeviceIdType.MESH
-CHUNKS = 2
+CHUNKS = 4
 
 HEAD_DIM = 88
 CTX_DEV = 32

time: 131 us -> 131 us (level)
  transfers between devices with their start and end apart: 3 -> 3, of which waited for: 1 -> 1; matrix products, arithmetic and copies ran while one was open for 13% -> 13% of each run, Pallas kernels for 21% -> 22%
where the time goes in v6:
time: 131 us; the launch traced here: 130 us
  Pallas kernels  83.4 us (64%)
  blocking collectives  17 us (13%)
  other arithmetic  14.3 us (11%)
  local copies, waits for them, and re-layouts  6.27 us (5%)
  starting transfers between devices  4.55 us (3%)
  matrix products  2.71 us (2%)
    pallas_call x2, Pallas kernels, gather_rows(): pl.pallas_call(functools.partial(gather_kernel, shards, with_seeds), out_...  49.4 us
    pallas_call x1, Pallas kernels, middle(): pl.pallas_call(functools.partial(middle_kernel, shards), out_shape=[jax.S...  33.9 us
    all_gather x1, blocking collectives, body(): lax.all_gather(head_grad, 'seq', axis=0, tiled=True).astype(jnp.float32)  17 us
    select_n x2, other arithmetic, both_of_dp(): jnp.where(first, block, other)  3.24 us
    add x1, other arithmetic, body(): MOMENTUM * target_out.astype(jnp.float32)  3.02 us
    ppermute x2, starting transfers between devices, swap(): return lax.ppermute(block, 'dp', [(0, 1), (1, 0)])  2.99 us
  transfers between devices with their start and end apart: 3, of which 1 were waited for; matrix products, arithmetic and copies ran while one was open for 13% of the time, Pallas kernels for 22%

profile of v6, /device:TPU:0, one launch (start us, length us, event | category | flops | bytes accessed | tf_op | source)
XLA Modules:
  0.0 130.3 jit_solution(1261076204375668182)
XLA Ops:
  0.6 2.0 %constant_dynamic-slice_fusion = (bf16[3,704,88]{2,1,0:T(8,128)(2,1)S(1)}, bf16[3,704,88]{2,1,0:T(8,128)(2,1)S(1)}) fusion(bf16[3,704,704]{2,1,0:T(8,128)(2,1)} %param.13, s32[]{:T(128)S(6)} %select_n.57, bf16[3,704,704]{2,1,0:T(8,128)(2,1)} %param.11), kind=kLoop, calls=%fused_computation.43 | loop fusion | bytes 1486852 | tf_op jit(solution)/shard_map/dynamic_slice | solution.py:459
  2.7 0.8 copy-done.4
  3.6 0.2 pad_maximum_fusion.1
  3.8 1.3 %copy.15 = bf16[6,704,88]{1,2,0:T(8,128)(2,1)} copy(bf16[6,704,88]{2,1,0:T(8,128)(2,1)S(1)} %pad_maximum_fusion.1) | data formatting | bytes 1486848 | tf_op jit(solution)/shard_map/concatenate | solution.py:461
  5.2 3.0 %collective-permute-start = (bf16[6,704,88]{1,2,0:T(8,128)(2,1)}, bf16[6,704,88]{1,2,0:T(8,128)(2,1)}, u32[]{:S(2)}, u32[]{:S(2)}) collective-permute-start(bf16[6,704,88]{1,2,0:T(8,128)(2,1)} %copy.15), channel_id=1, source_target_pairs={{0,1},{1,0},{2,3},{3,2},{4,5},{5,4},{6,7},{7,6},{8,9},{9,8},{10,11... | collective-permute-start | bytes 2230280 | tf_op jit(solution)/shard_map/ppermute | solution.py:431
  8.3 0.2 multiply_reduce_fusion
  8.6 0.8 convert_bitcast_fusion
  9.6 0.8 multiply_sine_fusion
  10.7 28.4 %gather_seeds.1 = (bf16[8,2,4,16,1408]{4,3,2,1,0:T(8,128)(2,1)S(1)}, s32[8,8,384]{2,1,0:T(8,128)S(1)}, bf16[1024,1408]{1,0:T(8,128)(2,1)}) custom-call(bf16[4,16,1408]{2,1,0:T(8,128)(2,1)S(1)} %multiply_convert_fusion.refs_0_, s32[8,384]{1,0:T(8,128)S(1)} %pad.4.refs_1_, f32[32,1408]{1,0:T(8,128)S(1)} %get-tuple-element.31.refs_2_, ...), custom_call_target="tpu_custom_call" | custom-call | tf_op jit(solution)/shard_map/gather_seeds/pallas_call | solution.py:249
  39.1 0.7 fusion.7
  40.1 1.0 reduce_window_sum.11
  41.4 2.1 %convolution_convert_fusion = bf16[8,32,1408]{2,1,0:T(8,128)(2,1)} fusion(bf16[8,128,1408]{2,1,0:T(8,128)(2,1)S(1)} %bitcast.22, s32[8,128]{1,0:T(8,128)S(1)} %broadcast_add_fusion, pred[8,128]{1,0:T(8,128)(4,1)} %get-tuple-element.21), kind=kOutput, calls=%fused_computation.1 | convolution fusion | flops 92700672 | bytes 3609600 | tf_op jit(solution)/shard_map/sck,skw->scw/dot_general | solution.py:498
  43.5 1.6 %copy.16 = bf16[6,704,88]{2,1,0:T(8,128)(2,1)S(1)} copy(bf16[6,704,88]{1,2,0:T(8,128)(2,1)} %collective-permute-done) | data formatting | bytes 1486848 | tf_op jit(solution)/shard_map/ppermute | solution.py:431
  45.1 1.5 %broadcast_select_fusion.3 = (bf16[6,704,88]{2,1,0:T(8,128)(2,1)S(1)}, bf16[6,704,88]{2,1,0:T(8,128)(2,1)S(1)}) fusion(bf16[6,704,88]{2,1,0:T(8,128)(2,1)S(1)} %copy.16, pred[]{:T(512)S(6)} %eq.36, bf16[3,704,88]{2,1,0:T(8,128)(2,1)} %copy-done.4, bf16[3,704,88]{2,1,0:T(8,128)(2,1)} %copy-done.5), kind=kLoop, calls=%fused_computation.8 | loop fusion | flops 1115136 | bytes 2973697 | tf_op jit(solution)/shard_map/jit(_where)/select_n | solution.py:441
  46.7 1.8 %pad_maximum_fusion.refs_3_ = bf16[6,1408,88]{2,1,0:T(8,128)(2,1)} fusion(bf16[6,704,88]{2,1,0:T(8,128)(2,1)S(1)} %get-tuple-element.25, bf16[6,704,88]{2,1,0:T(8,128)(2,1)S(1)} %get-tuple-element.24), kind=kLoop, calls=%fused_computation.3 | loop fusion | flops 2973696 | bytes 2973696 | tf_op jit(solution)/shard_map/concatenate | solution.py:440
  48.4 1.3 collective-permute-done.1.refs_6_
  49.7 33.9 %middle.1 = (bf16[64,1408]{1,0:T(8,128)(2,1)S(1)}, bf16[8,128,88]{2,1,0:T(8,128)(2,1)S(1)}) custom-call(bf16[8,128,1408]{2,1,0:T(8,128)(2,1)} %bitcast.23, bf16[8,128,1408]{2,1,0:T(8,128)(2,1)} %bitcast.28, bf16[256,1408]{1,0:T(8,128)(2,1)S(1)} %bitcast.25, bf16[6,1408,88]{2,1,0:T(8,128)(2,1)} %pad_maximum_fusion.refs_3_, bf16[704,1408]{1,0:T(8,128)(2,1)S(1)} %copy-done.1, ...), custom_call_target="tpu_custom_call" | custom-call | tf_op jit(solution)/shard_map/middle/pallas_call | solution.py:385
  83.6 21.0 %gather_rows.1 = bf16[8,2,4,16,1408]{4,3,2,1,0:T(8,128)(2,1)S(1)} custom-call(bf16[4,16,1408]{2,1,0:T(8,128)(2,1)S(1)} %bitcast.27), custom_call_target="tpu_custom_call" | custom-call | tf_op jit(solution)/shard_map/gather_rows/pallas_call | solution.py:249
  104.7 0.6 convolution_convert_fusion.1
  105.4 1.6 %collective-permute-start.2 = (bf16[88,704]{1,0:T(8,128)(2,1)S(1)}, bf16[88,704]{1,0:T(8,128)(2,1)S(1)}, u32[]{:S(2)}, u32[]{:S(2)}) collective-permute-start(bf16[88,704]{1,0:T(8,128)(2,1)S(1)} %broadcast_select_fusion.4), channel_id=1, source_target_pairs={{0,1},{1,0},{2,3},{3,2},{4,5},{5,4},{6,7},{7,6},{8,9},{9,8},{10,11... | collective-permute-start | bytes 371720 | tf_op jit(solution)/shard_map/ppermute | solution.py:575
  106.9 1.7 %broadcast_select_fusion.1 = (bf16[704,704]{1,0:T(8,128)(2,1)S(1)}, bf16[704,704]{1,0:T(8,128)(2,1)S(1)}) fusion(bf16[704,704]{1,0:T(8,128)(2,1)} %refs_5_.1, bf16[704,704]{1,0:T(8,128)(2,1)} %collective-permute-done.1.refs_6_, pred[]{:T(512)S(6)} %eq.36), kind=kLoop, calls=%fused_computation.6 | loop fusion | flops 991232 | bytes 3964929 | tf_op jit(solution)/shard_map/jit(_where)/select_n | solution.py:441
  108.6 3.0 %multiply_add_fusion = f32[704,1408]{1,0:T(8,128)} fusion(bf16[704,1408]{1,0:T(8,128)(2,1)S(1)} %copy-done.1, bf16[704,704]{1,0:T(8,128)(2,1)S(1)} %get-tuple-element.23, bf16[704,704]{1,0:T(8,128)(2,1)S(1)} %get-tuple-element.22), kind=kLoop, calls=%fused_computation | loop fusion | flops 7929856 | bytes 7929856 | tf_op jit(solution)/shard_map/add | solution.py:583
  111.8 17.0 %all_gather.3 = bf16[704,704]{1,0:T(8,128)(2,1)S(1)} all-gather(bf16[88,704]{1,0:T(8,128)(2,1)S(1)} %add_convert_fusion), channel_id=1, replica_groups=mesh['seq'=8,'grp'=2,'dp'=2] {'seq'}, dimensions={0}, use_global_device_ids=true | all-gather | bytes 1115136 | tf_op jit(solution)/shard_map/all_gather | solution.py:579
  128.8 1.5 %convert_element_type.84 = f32[704,704]{1,0:T(8,128)} convert(bf16[704,704]{1,0:T(8,128)(2,1)S(1)} %all_gather.3) | non-fusion elementwise | flops 495616 | bytes 2973696 | tf_op jit(solution)/shard_map/convert_element_type | solution.py:579
  (50 shorter events, 1.7 us)
Async XLA Ops:
  2.6 0.8 copy-start.4
  2.6 1.0 copy-start.5
  2.6 5.5 %copy-start.6 = (bf16[1,128,1408]{2,1,0:T(8,128)(2,1)S(1)}, bf16[1,128,1408]{2,1,0:T(8,128)(2,1)}, u32[]{:S(2)}) copy-start(bf16[1,128,1408]{2,1,0:T(8,128)(2,1)} %param.8) | copy-start | bytes 1081348
  3.6 5.9 %copy-start.8 = (s32[1,192]{1,0:T(1,128)S(1)}, s32[1,192]{1,0:T(1,128)}, u32[]{:S(2)}) copy-start(s32[1,192]{1,0:T(1,128)} %param.10) | copy-start | bytes 2308
  3.6 5.9 %copy-start.9 = (s32[1,128]{1,0:T(1,128)S(1)}, s32[1,128]{1,0:T(1,128)}, u32[]{:S(2)}) copy-start(s32[1,128]{1,0:T(1,128)} %param.9) | copy-start | bytes 1540
  3.6 5.9 %copy-start.7 = (f32[1408]{0:T(1024)S(1)}, f32[1408]{0:T(1024)}, u32[]{:S(2)}) copy-start(f32[1408]{0:T(1024)} %param.15) | copy-start | bytes 16900
  5.2 38.3 %collective-permute-start = (bf16[6,704,88]{1,2,0:T(8,128)(2,1)}, bf16[6,704,88]{1,2,0:T(8,128)(2,1)}, u32[]{:S(2)}, u32[]{:S(2)}) collective-permute-start(bf16[6,704,88]{1,2,0:T(8,128)(2,1)} %copy.15), channel_id=1, source_target_pairs={{0,1},{1,0},{2,3},{3,2},{4,5},{5,4},{6,7},{7,6},{8,9},{9,8},{10,11... | collective-permute-start | bytes 2230280 | tf_op jit(solution)/shard_map/ppermute | solution.py:431
  8.1 41.6 %collective-permute-start.1 = (bf16[704,704]{1,0:T(8,128)(2,1)}, bf16[704,704]{1,0:T(8,128)(2,1)}, u32[]{:S(2)}, u32[]{:S(2)}) collective-permute-start(bf16[704,704]{1,0:T(8,128)(2,1)} %refs_5_.1), channel_id=1, source_target_pairs={{0,1},{1,0},{2,3},{3,2},{4,5},{5,4},{6,7},{7,6},{8,9},{9,8},{10,11... | collective-permute-start | bytes 2973704 | tf_op jit(solution)/shard_map/ppermute | solution.py:431
  39.1 4.4 %copy-start = (bf16[8,2,4,16,1408]{4,3,2,1,0:T(8,128)(2,1)}, bf16[8,2,4,16,1408]{4,3,2,1,0:T(8,128)(2,1)S(1)}, u32[]{:S(2)}) copy-start(bf16[8,2,4,16,1408]{4,3,2,1,0:T(8,128)(2,1)S(1)} %get-tuple-element.11) | copy-start | bytes 8650756
  46.6 3.1 %copy-start.1 = (bf16[704,1408]{1,0:T(8,128)(2,1)S(1)}, bf16[704,1408]{1,0:T(8,128)(2,1)}, u32[]{:S(2)}) copy-start(bf16[704,1408]{1,0:T(8,128)(2,1)} %refs_4_.1) | copy-start | bytes 5947396
  46.6 3.0 %copy-start.2 = (bf16[8,32,1408]{2,1,0:T(8,128)(2,1)S(1)}, bf16[8,32,1408]{2,1,0:T(8,128)(2,1)}, u32[]{:S(2)}) copy-start(bf16[8,32,1408]{2,1,0:T(8,128)(2,1)} %convolution_convert_fusion) | copy-start | bytes 2162692
  46.6 3.0 %copy-start.3 = (f32[64,1408]{1,0:T(8,128)S(1)}, f32[64,1408]{1,0:T(8,128)}, u32[]{:S(2)}) copy-start(f32[64,1408]{1,0:T(8,128)} %get-tuple-element.26.refs_7_) | copy-start | bytes 1081348
  105.4 6.3 %collective-permute-start.2 = (bf16[88,704]{1,0:T(8,128)(2,1)S(1)}, bf16[88,704]{1,0:T(8,128)(2,1)S(1)}, u32[]{:S(2)}, u32[]{:S(2)}) collective-permute-start(bf16[88,704]{1,0:T(8,128)(2,1)S(1)} %broadcast_select_fusion.4), channel_id=1, source_target_pairs={{0,1},{1,0},{2,3},{3,2},{4,5},{5,4},{6,7},{7,6},{8,9},{9,8},{10,11... | collective-permute-start | bytes 371720 | tf_op jit(solution)/shard_map/ppermute | solution.py:575
